TPU v7x, 32 devices: a whole 2x2x4 slice. The times are simulated.
32 devices in a mesh: dp: 2 (over y), fsdp: 4 (over x, core), tensor: 4 (over z).
Axes of the slice: x: 2, y: 2, z: 4, core: 2. Of those that a mesh axis runs over, the one named last changes fastest.
Arguments:
- activations: bfloat16 [1024, 8192], P(('dp', 'fsdp'), 'tensor'), may hold values from -6 to 6
- cotangent: bfloat16 [1024, 8192], P(('dp', 'fsdp'), 'tensor'), may hold values from -6 to 6
- up_tiles: bfloat16 [1024, 128, 128], P(('fsdp', 'tensor')), may hold values from -0.1875 to 0.1875
- down_tiles: bfloat16 [1024, 128, 128], P(('fsdp', 'tensor')), may hold values from -0.125 to 0.125
- up_rows: int32 [256, 4], P(None, 'tensor'), may hold values from 0 to 63, as said below
- up_cols: int32 [256, 4], P(None, 'tensor'), may hold values from 0 to 31, as said below
- down_rows: int32 [256, 4], P(None, 'tensor'), may hold values from 0 to 31, as said below
- down_cols: int32 [256, 4], P(None, 'tensor'), may hold values from 0 to 63, as said below
Outputs:
- output: bfloat16 [1024, 8192], P(('dp', 'fsdp'), 'tensor')
- input_grad: bfloat16 [1024, 8192], P(('dp', 'fsdp'), 'tensor')
- up_grad: float32 [1024, 128, 128], P(('fsdp', 'tensor'))
- down_grad: float32 [1024, 128, 128], P(('fsdp', 'tensor'))
Inputs may be any that keep to these rules, and one draw needn't show every extreme that they name: `up_rows`: within a column, the up tiles of one hidden-unit block name distinct feature blocks. `up_cols`: every value occurs exactly 8 times in each column. `down_rows`: every value occurs exactly 8 times in each column. `down_cols`: within a column, the down tiles of one hidden-unit block name distinct feature blocks.
All inputs are finite; a program needn't handle non-finite values.
Results may differ from a plain program's by a relative error of at most 0.018.
Values may be sent and summed in bfloat16 or wider, within the bound.
A program may use at most 128 MiB of HBM per device.

v0:
```python
import functools

import jax
import jax.numpy as jnp
from jax import lax
from jax.experimental import pallas as pl
from jax.experimental.pallas import tpu as pltpu
from jax.sharding import PartitionSpec as P

MESH = pl.DeviceIdType.MESH
COL_TILES = 8
PIECES = 16
CHUNKS = 2
WEIGHT_CHUNKS = 4
PARTS = 4

SHARD_TIME = 11.3
PIECE_TIME = 2.8
WEIGHT_TIME = 5.6

inv_root_two = 0.7071067811865476
inv_root_tau = 0.3989422804014327


def gelu_parts(values):
    normal_cdf = 0.5 * (1.0 + lax.erf(values * inv_root_two))
    density = inv_root_tau * jnp.exp(-0.5 * values * values)
    return (values * normal_cdf, normal_cdf + values * density)


def mm(a, b, ca, cb):
    return lax.dot_general(a, b, (((ca,), (cb,)), ((), ())), preferred_element_type=jnp.float32)


def wide(blocks, axis):
    return jnp.concatenate(blocks, axis=axis)


def remote(src, dst, send_sem, recv_sem, where):
    return pltpu.make_async_remote_copy(
        src_ref=src, dst_ref=dst, send_sem=send_sem, recv_sem=recv_sem,
        device_id=where, device_id_type=MESH,
    )


def place(sizes):
    n, chips, replicas = sizes
    z = lax.axis_index("tensor")
    f = lax.axis_index("fsdp")
    y = lax.axis_index("dp")
    return z, f // 2, f % 2, y


def enter(sizes):
    n, chips, replicas = sizes
    z, r, c, y = place(sizes)
    barrier = pltpu.get_barrier_semaphore()

    def greet(where):
        pl.semaphore_signal(barrier, inc=1, device_id=where, device_id_type=MESH)

    @pl.when(z < n - 1)
    def _():
        greet({"tensor": z + 1})

    @pl.when(z > 0)
    def _():
        greet({"tensor": z - 1})

    greet({"fsdp": r * 2 + 1 - c})
    for d in range(1, chips):
        greet({"fsdp": lax.rem(r + d, chips) * 2 + c})
    for e in range(1, replicas):
        greet({"dp": lax.rem(y + e, replicas)})
    sides = jnp.where(z < n - 1, 1, 0) + jnp.where(z > 0, 1, 0)
    pl.semaphore_wait(barrier, sides + 1 + (chips - 1) + (replicas - 1))


def block_kernel(
    sizes, uo, uf, do, df, up_rows, up_cols, down_rows, down_cols,
    pair_order_u, pair_near_u, pair_first_u, last_u, pair_order_d, pair_near_d, pair_first_d, last_d,
    act, cot, up, down,
    out, inp, ga_u, ga_d, gb_u, gb_d,
    x_all, xt_own, xt_mate, cot_own, cot_mate, u_all, d_all, hidden, ht_own, ht_mate, slope,
    pg_own, pg_mate, run, acc, parts_o, parts_i, held_r, held_l, stage, x_in,
    load_sem, zs_sem, zr_sem, ms_sem, mr_sem, ts_sem, tr_sem, ws_sem, wr_sem, ys_sem, yr_sem, cs_sem, cr_sem,
    os_sem, or_sem, hs_sem, hr_sem, gs_sem, gr_sem, ls_sem, lr_sem, xs_sem, xr_sem, es_sem, er_sem, keep_sem,
):
    n, chips, replicas = sizes
    z, r, c, y = place(sizes)
    f = r * 2 + c
    blocks = act.shape[1] // 128
    per = up.shape[0]
    part = per // replicas
    total_tiles = u_all.shape[0]
    hidden_blocks = slope.shape[0]
    chunk = blocks // CHUNKS
    weight_chunks = min(WEIGHT_CHUNKS, part)
    weight_size = part // weight_chunks
    pieces = min(PIECES, per)
    size = per // pieces
    span = hidden_blocks // PARTS
    features = (x_all, cot_own)
    weights = ((up, u_all), (down, d_all))
    mate = {"fsdp": r * 2 + 1 - c}

    loads = ([], [])
    for a, (src, full) in enumerate(((act, x_all), (cot, cot_own))):
        for b in range(blocks):
            copy = pltpu.make_async_copy(
                src.at[:, pl.ds(b * 128, 128)], full.at[z * blocks + b], load_sem.at[a, b]
            )
            copy.start()
            loads[a].append(copy)
    weight_loads = []
    for a, (src, full) in enumerate(weights):
        copy = pltpu.make_async_copy(src, full.at[pl.ds(f * per, per)], load_sem.at[2 + a, 0])
        copy.start()
        weight_loads.append(copy)
    hidden[hidden_blocks] = jnp.zeros(hidden.shape[1:], hidden.dtype)
    pg_own[hidden_blocks] = jnp.zeros(pg_own.shape[1:], pg_own.dtype)
    enter(sizes)

    def shard(full, s, k):
        return full.at[pl.ds(s * blocks + k * chunk, chunk)]

    def line(a, s, k, way):
        piece = shard(features[a], z - way * s, k)
        w = 0 if way > 0 else 1
        return remote(
            piece, piece, zs_sem.at[a, w, s, k], zr_sem.at[a, w, s, k], {"tensor": z + way}
        )

    def can_send(way):
        return z < n - 1 if way > 0 else z > 0

    def has(s, way):
        return z - s >= 0 if way > 0 else z + s <= n - 1

    def z_start(a):
        for k in range(CHUNKS):
            for way in (1, -1):

                @pl.when(can_send(way))
                def _():
                    line(a, 0, k, way).start()

    def mate_chunk(a, s, k, way):
        w = 0 if way > 0 else 1
        src, dst = ((xt_own, xt_mate), (cot_own, cot_mate))[a]
        sems = ((ts_sem, tr_sem), (ms_sem, mr_sem))[a]
        return remote(
            shard(src, z - way * s, k), shard(dst, z - way * s, k),
            sems[0].at[w, s, k], sems[1].at[w, s, k], mate,
        )

    def turn(s, k, way):
        first = (z - way * s) * blocks + k * chunk

        @pl.loop(0, chunk)
        def _(b):
            xt_own[first + b] = x_all[first + b].T

        mate_chunk(0, s, k, way).start()

    def z_event(a, s, k):
        for way in (1, -1):

            @pl.when(has(s, way))
            def _():
                line(a, s - 1, k, way).wait_recv()
                if s < n - 1:

                    @pl.when(can_send(way))
                    def _():
                        line(a, s, k, way).start()

                if a == 1:
                    mate_chunk(1, s, k, way).start()

    def turn_event(s, k):
        for way in (1, -1):

            @pl.when(has(s, way))
            def _():
                turn(s, k, way)

    def mate_chunks(a, act_on):
        for k in range(CHUNKS):
            act_on(mate_chunk(a, 0, k, 1))
            for s in range(1, n):
                for way in (1, -1):

                    @pl.when(has(s, way))
                    def _():
                        act_on(mate_chunk(a, s, k, way))

    def tile_range(full, r_of, q, k):
        return full.at[pl.ds((r_of * 2 + c) * per + q * part + k * weight_size, weight_size)]

    def from_chip(d):
        return lax.rem(r - d + chips, chips)

    def w_copy(a, d, k):
        src = weights[a][0].at[pl.ds(y * part + k * weight_size, weight_size)]
        return remote(
            src, tile_range(weights[a][1], r, y, k), ws_sem.at[a, d, k], wr_sem.at[a, d, k],
            {"fsdp": lax.rem(r + d, chips) * 2 + c},
        )

    def y_copy(a, d, e, k):
        piece = tile_range(weights[a][1], from_chip(d), y, k)
        return remote(
            piece, piece, ys_sem.at[a, d, e, k], yr_sem.at[a, d, e, k],
            {"dp": lax.rem(y + e, replicas)},
        )

    def core_copy(a, d, e, k):
        piece = tile_range(weights[a][1], from_chip(d), lax.rem(y - e + replicas, replicas), k)
        return remote(piece, piece, cs_sem.at[a, d, e, k], cr_sem.at[a, d, e, k], mate)

    def own_core(a):
        return remote(
            weights[a][0], weights[a][1].at[pl.ds(f * per, per)], os_sem.at[a], or_sem.at[a], mate
        )

    def w_event(a, k):
        for d in range(1, chips):
            w_copy(a, d, k).wait_recv()
            for e in range(1, replicas):
                y_copy(a, d, e, k).start()
            core_copy(a, d, 0, k).start()

    def y_event(a, k):
        for d in range(1, chips):
            for e in range(1, replicas):
                y_copy(a, d, e, k).wait_recv()
                core_copy(a, d, e, k).start()

    def weights_in(a):
        weight_loads[a].wait()
        own_core(a).wait_recv()
        for d in range(1, chips):
            for e in range(replicas):
                for k in range(weight_chunks):
                    core_copy(a, d, e, k).wait_recv()

    def hidden_mate(g):
        at = pl.ds(g * span, span)
        return remote(ht_own.at[at], ht_mate.at[at], hs_sem.at[g], hr_sem.at[g], mate)

    def hidden_part(g):
        @pl.loop(g * span, (g + 1) * span)
        def _(h):
            spots = [h * COL_TILES + k for k in range(COL_TILES)]
            pre = mm(
                wide([x_all[uf[i]] for i in spots], 1), wide([u_all[uo[i]] for i in spots], 0), 1, 0
            )
            value, tangent = gelu_parts(pre)
            value = value.astype(jnp.bfloat16)
            hidden[h] = value
            ht_own[h] = value.T
            slope[h] = tangent

        hidden_mate(g).start()

    def grad_mate(g):
        at = pl.ds(g * span, span)
        return remote(pg_own.at[at], pg_mate.at[at], gs_sem.at[g], gr_sem.at[g], mate)

    def slope_part(g):
        @pl.loop(g * span, (g + 1) * span)
        def _(h):
            spots = [h * COL_TILES + k for k in range(COL_TILES)]
            value = mm(
                wide([cot_own[df[i]] for i in spots], 1), wide([d_all[do[i]] for i in spots], 1), 1, 1
            )
            pg_own[h] = (value * slope[h]).astype(jnp.bfloat16)

        grad_mate(g).start()

    parts = (parts_o, parts_i)
    outs = (out, inp)
    held = (held_r, held_l)
    pair_width = 4

    def run_part(a, g):
        order, near, fresh = (
            (pair_order_d, pair_near_d, pair_first_d) if a == 0 else (pair_order_u, pair_near_u, pair_first_u)
        )
        left, right, cut = (hidden, d_all, 0) if a == 0 else (pg_own, u_all, 1)
        steps = run.shape[0] // PARTS // pair_width
        if g == 0:
            acc[...] = jnp.zeros_like(acc)

        @pl.loop(g * steps, (g + 1) * steps)
        def _(b):
            total = acc[...]
            for i in [b * pair_width + k for k in range(pair_width)]:
                product = mm(
                    wide([left[near[2 * i]], left[near[2 * i + 1]]], 1),
                    wide([right[order[2 * i]], right[order[2 * i + 1]]], cut), 1, cut,
                )
                total = jnp.where(fresh[i] == 1, 0.0, total) + product
                run[i] = total.astype(jnp.bfloat16)
            acc[...] = total

    def part_shard(ref, s):
        return ref.at[pl.ds(s * blocks, blocks)]

    def fold(a, i, way, source):
        s = n - 1 - i if way > 0 else i
        k = 0 if way > 0 else 1
        src = part_shard(parts[a], s) if source else held[k].at[a, i]
        return remote(
            src, held[k].at[a, i], ls_sem.at[a, k, i], lr_sem.at[a, k, i], {"tensor": z + way}
        )

    def edge(way):
        return z == 0 if way > 0 else z == n - 1

    def sends(i, way):
        return n - 1 - i > z if way > 0 else i < z

    def settle(a):
        last = last_d if a == 0 else last_u
        target = parts[a]

        @pl.loop(0, target.shape[0])
        def _(b):
            spot = last[b]
            found = run[jnp.maximum(spot, 0)]
            target[b] = jnp.where(spot >= 0, found, jnp.zeros_like(found))

        for i in range(n - 1):
            for way in (1, -1):

                @pl.when(edge(way))
                def _():
                    fold(a, i, way, True).start()

    def add_into(target, terms):
        @pl.loop(0, target.shape[0])
        def _(b):
            total = terms[0][b].astype(jnp.float32)
            for term_of in terms[1:]:
                total += term_of[b].astype(jnp.float32)
            target[b] = total.astype(target.dtype)

    def fold_event(a, t):
        for way in (1, -1):
            i = t - z if way > 0 else t - (n - 1 - z)
            s = n - 1 - i if way > 0 else i
            k = 0 if way > 0 else 1
            on_way = jnp.logical_and(i >= 0, sends(i, way))

            @pl.when(jnp.logical_and(on_way, jnp.logical_not(edge(way))))
            def _():
                fold(a, i, way, False).wait_recv()
                add_into(held[k].at[a, i], (held[k].at[a, i], part_shard(parts[a], s)))
                fold(a, i, way, False).start()

    def finish(a):
        mine = part_shard(parts[a], z)
        target = outs[a]

        def write(terms):
            for b in range(blocks):
                total = terms[0][b].astype(jnp.float32)
                for term_of in terms[1:]:
                    total += term_of[b].astype(jnp.float32)
                target[:, pl.ds(b * 128, 128)] = total.astype(target.dtype)

        @pl.when(z > 0)
        def _():
            fold(a, n - 1 - z, 1, False).wait_recv()

        @pl.when(z < n - 1)
        def _():
            fold(a, z, -1, False).wait_recv()

        @pl.when(z == 0)
        def _():
            write((mine, held_l.at[a, z]))

        @pl.when(z == n - 1)
        def _():
            write((mine, held_r.at[a, n - 1 - z]))

        @pl.when(jnp.logical_and(z > 0, z < n - 1))
        def _():
            write((mine, held_r.at[a, n - 1 - z], held_l.at[a, z]))

    sums = (ga_d, ga_u)
    others = (gb_d, gb_u)

    def term(a, j):
        if a == 0:
            at, to = down_rows[j], down_cols[j]
            return mm(wide([ht_own[at], ht_mate[at]], 1), wide([cot_own[to], cot_mate[to]], 0), 1, 0)
        at, to = up_rows[j], up_cols[j]
        return mm(wide([xt_own[at], xt_mate[at]], 1), wide([pg_own[to], pg_mate[to]], 0), 1, 0)

    def first_tile(q, k):
        return (q * 2 + c) * per + k * size

    def x_copy(a, k, d):
        q = lax.rem(r + d, chips)
        at = pl.ds(k * size, size)
        return remote(
            stage.at[a, d - 1, at], x_in.at[a, d - 1, at], xs_sem.at[a, k, d], xr_sem.at[a, k, d],
            {"fsdp": q * 2 + c},
        )

    def hand_over(a):
        @pl.loop(0, pieces)
        def _(k):
            for d in range(1, chips):
                first = first_tile(lax.rem(r + d, chips), k)
                values = [term(a, first + i) for i in range(size)]
                for i in range(size):
                    stage[a, d - 1, k * size + i] = values[i].astype(jnp.bfloat16)
                x_copy(a, k, d).start()

    def done_piece(a, k):
        return x_in.at[a, 0, pl.ds(k * size, size)]

    def e_copy(a, k, e):
        return remote(
            done_piece(a, k), others[a].at[e - 1, pl.ds(k * size, size)],
            es_sem.at[a, k, e], er_sem.at[a, k, e], {"dp": lax.rem(y + e, replicas)},
        )

    def keep_copy(a, k):
        return pltpu.make_async_copy(
            done_piece(a, k), sums[a].at[pl.ds(k * size, size)], keep_sem.at[a, k]
        )

    def x_event(a, k):
        first = first_tile(r, k)
        values = [term(a, first + i) for i in range(size)]
        for d in range(1, chips):
            x_copy(a, k, d).wait_recv()
        for i in range(size):
            total = values[i]
            for d in range(1, chips):
                total += x_in[a, d - 1, k * size + i].astype(jnp.float32)
            x_in[a, 0, k * size + i] = total.astype(jnp.bfloat16)
        for e in range(1, replicas):
            e_copy(a, k, e).start()
        keep_copy(a, k).start()

    plan = []

    def at(time, work, *args):
        plan.append((time, functools.partial(work, *args)))

    def start_all():
        for copy in loads[0]:
            copy.wait()
        z_start(0)
        for a in range(2):
            for k in range(weight_chunks):
                for d in range(1, chips):
                    w_copy(a, d, k).start()
        for a in range(2):
            own_core(a).start()
        for k in range(CHUNKS):
            turn(0, k, 1)
        for copy in loads[1]:
            copy.wait()
        for k in range(CHUNKS):
            mate_chunk(1, 0, k, 1).start()

    at(0.0, start_all)
    chunk_time = SHARD_TIME / CHUNKS
    for s in range(1, n):
        for k in range(CHUNKS):
            when = 2.0 + ((s - 1) * CHUNKS + k + 1) * chunk_time
            at(when, z_event, 0, s, k)
            at(when + 0.1, turn_event, s, k)
    act_in = 2.0 + (n - 1) * SHARD_TIME
    at(2.05 + max(n - 2, 0) * SHARD_TIME, z_start, 1)
    for a in range(2):
        for k in range(weight_chunks):
            when = 2.2 + (a * weight_chunks + k + 1) * WEIGHT_TIME
            at(when, w_event, a, k)
            at(when + 1.2 * WEIGHT_TIME, y_event, a, k)
    up_in = 2.3 + (weight_chunks + 1.2) * WEIGHT_TIME
    down_in = 2.3 + (2 * weight_chunks + 1.2) * WEIGHT_TIME
    at(up_in + 2.0, weights_in, 0)
    at(down_in + 2.0, weights_in, 1)
    hidden_from = max(act_in, up_in + 2.0) + 0.5
    for g in range(PARTS):
        at(hidden_from + 3.0 * g, hidden_part, g)
    out_from = max(hidden_from + 3.0 * PARTS, down_in + 2.0) + 0.5
    for g in range(PARTS):
        at(out_from + 2.0 * g, run_part, 0, g)
    out_settle = out_from + 2.0 * PARTS
    at(out_settle, settle, 0)
    for s in range(1, n):
        for k in range(CHUNKS):
            at(act_in + ((s - 1) * CHUNKS + k + 1) * chunk_time, z_event, 1, s, k)
    cot_in = max(act_in + (n - 1) * SHARD_TIME, out_settle) + 1.0

    def cot_ready():
        mate_chunks(1, lambda copy: copy.wait_recv())
        for g in range(PARTS):
            hidden_mate(g).wait_recv()

    at(cot_in, cot_ready)
    at(cot_in + 0.1, hand_over, 0)
    slope_from = cot_in + 7.0
    for g in range(PARTS):
        at(slope_from + 2.5 * g, slope_part, g)

    def grads_ready():
        mate_chunks(0, lambda copy: copy.wait_recv())
        for g in range(PARTS):
            grad_mate(g).wait_recv()

    up_from = slope_from + 2.5 * PARTS
    at(up_from, grads_ready)
    at(up_from + 0.1, hand_over, 1)
    inp_from = up_from + 7.0
    for g in range(PARTS):
        at(inp_from + 2.0 * g, run_part, 1, g)
    inp_settle = inp_from + 2.0 * PARTS
    at(inp_settle, settle, 1)
    for a, start in enumerate((out_settle, inp_settle)):
        for t in range(1, n - 1):
            at(start + 1.0 + t * SHARD_TIME, fold_event, a, t)
        at(start + 3.0 + (n - 1) * SHARD_TIME, finish, a)
    for a in range(2):
        for k in range(pieces):
            when = cot_in + 4.0 + PIECE_TIME * (a * pieces + k + 1)
            at(max(when, up_from + 0.2) if a else when, x_event, a, k)

    plan.sort(key=lambda item: item[0])
    for _, work in plan:
        work()

    for a in range(2):
        mate_chunks(a, lambda copy: copy.wait_send())
        own_core(a).wait_send()
        for d in range(1, chips):
            for k in range(weight_chunks):
                w_copy(a, d, k).wait_send()
                for e in range(replicas):
                    core_copy(a, d, e, k).wait_send()
                for e in range(1, replicas):
                    y_copy(a, d, e, k).wait_send()
        for way in (1, -1):
            for s in range(n - 1):

                @pl.when(jnp.logical_and(can_send(way), has(s, way)))
                def _():
                    for k in range(CHUNKS):
                        line(a, s, k, way).wait_send()

        for i in range(n - 1):
            for way in (1, -1):

                @pl.when(sends(i, way))
                def _():
                    fold(a, i, way, False).wait_send()

    for g in range(PARTS):
        hidden_mate(g).wait_send()
        grad_mate(g).wait_send()
    for a in range(2):

        @pl.loop(0, pieces)
        def _(k):
            for d in range(1, chips):
                x_copy(a, k, d).wait_send()
            keep_copy(a, k).wait()
            for e in range(1, replicas):
                e_copy(a, k, e).wait()


def run_block(sizes, tables, activations, cotangent, up_tiles, down_tiles):
    n, chips, replicas = sizes
    rows, features = activations.shape
    blocks = features // 128
    per = up_tiles.shape[0]
    total_tiles = 2 * chips * per
    hidden_blocks = total_tiles // COL_TILES
    model_blocks = n * blocks
    pairs = (total_tiles + model_blocks) // 2
    part = per // replicas
    weight_chunks = min(WEIGHT_CHUNKS, part)
    pieces = min(PIECES, per)
    kind = jnp.bfloat16
    dma = pltpu.SemaphoreType.DMA
    vmem = pl.BlockSpec(memory_space=pltpu.VMEM)
    smem = pl.BlockSpec(memory_space=pltpu.SMEM)
    anywhere = pl.BlockSpec(memory_space=pl.ANY)

    def held(*shape):
        return pltpu.VMEM(shape + (rows, 128), kind)

    def twice(*shape):
        return [dma(shape), dma(shape)]

    return pl.pallas_call(
        functools.partial(block_kernel, sizes),
        out_shape=(
            [jax.ShapeDtypeStruct((rows, features), kind)] * 2
            + [jax.ShapeDtypeStruct((per, 128, 128), kind)] * 2
            + [jax.ShapeDtypeStruct((replicas - 1, per, 128, 128), kind)] * 2
        ),
        in_specs=[smem] * len(tables) + [anywhere] * 4,
        out_specs=[vmem] * 2 + [anywhere] * 4,
        scratch_shapes=[
            held(model_blocks),
            pltpu.VMEM((model_blocks, 128, rows), kind),
            pltpu.VMEM((model_blocks, 128, rows), kind),
            held(model_blocks),
            held(model_blocks),
            pltpu.VMEM((total_tiles, 128, 128), kind),
            pltpu.VMEM((total_tiles, 128, 128), kind),
            held(hidden_blocks + 1),
            pltpu.VMEM((hidden_blocks, 128, rows), kind),
            pltpu.VMEM((hidden_blocks, 128, rows), kind),
            pltpu.VMEM((hidden_blocks, rows, 128), jnp.float32),
            held(hidden_blocks + 1),
            held(hidden_blocks),
            held(pairs),
            pltpu.VMEM((rows, 128), jnp.float32),
            held(model_blocks),
            held(model_blocks),
            held(2, n - 1, blocks),
            held(2, n - 1, blocks),
            pltpu.VMEM((2, chips - 1, per, 128, 128), kind),
            pltpu.VMEM((2, chips - 1, per, 128, 128), kind),
            dma((4, blocks)),
            *twice(2, 2, n, CHUNKS),
            *twice(2, n, CHUNKS),
            *twice(2, n, CHUNKS),
            *twice(2, chips, weight_chunks),
            *twice(2, chips, replicas, weight_chunks),
            *twice(2, chips, replicas, weight_chunks),
            *twice(2),
            *twice(PARTS),
            *twice(PARTS),
            *twice(2, 2, n),
            *twice(2, pieces, chips),
            *twice(2, pieces, replicas),
            dma((2, pieces)),
        ],
        compiler_params=pltpu.CompilerParams(
            collective_id=0, has_side_effects=True, vmem_limit_bytes=67043328
        ),
        name="block_all",
    )(*tables, activations, cotangent, up_tiles, down_tiles)


def total_kernel(ga_u, gb_u, ga_d, gb_d, up_grad, down_grad):
    for one, more, target in ((ga_u, gb_u, up_grad), (ga_d, gb_d, down_grad)):
        total = one[...].astype(jnp.float32)
        for e in range(more.shape[0]):
            total += more[e].astype(jnp.float32)
        target[...] = total


def totals(ga_u, gb_u, ga_d, gb_d):
    per = ga_u.shape[0]
    step = min(8, per)
    one = pl.BlockSpec((step, 128, 128), lambda i: (i, 0, 0))
    more = pl.BlockSpec((gb_u.shape[0], step, 128, 128), lambda i: (0, i, 0, 0))
    return pl.pallas_call(
        total_kernel,
        grid=(per // step,),
        out_shape=[jax.ShapeDtypeStruct(ga_u.shape, jnp.float32)] * 2,
        in_specs=[one, more, one, more],
        out_specs=[one, one],
        name="totals",
    )(ga_u, gb_u, ga_d, gb_d)


def tables_of(near, far, model_blocks):
    count = near.shape[0]
    near_size = count // COL_TILES + 1
    at = lax.iota(jnp.int32, count)
    before = at[:, None] < at[None, :]
    equal = far[:, None] == far[None, :]
    spot = near * COL_TILES + jnp.sum(((near[:, None] == near[None, :]) & before).astype(jnp.int32), axis=0)
    here = spot[:, None] == at[None, :]
    packed = jnp.sum(jnp.where(here, (at * model_blocks + far)[:, None], 0), axis=0)
    rank = jnp.sum((equal & before).astype(jnp.int32), axis=0)
    often = jnp.sum(equal.astype(jnp.int32), axis=0)
    takes = 1 + jnp.where((rank == often - 1) & (often % 2 == 1), 1, 0)
    place_of = rank + jnp.sum(jnp.where(far[:, None] < far[None, :], takes[:, None], 0), axis=0)
    there = place_of[:, None] == lax.iota(jnp.int32, count + model_blocks)[None, :]
    code = ((at * near_size + near) * 2 + (rank == 0)) - (near_size - 1) * 2
    pair_code = jnp.sum(jnp.where(there, code[:, None], 0), axis=0) + (near_size - 1) * 2
    block = lax.iota(jnp.int32, model_blocks)
    matches = far[:, None] == block[None, :]
    until = jnp.sum(jnp.where(far[:, None] <= block[None, :], takes[:, None], 0), axis=0)
    last = jnp.where(jnp.any(matches, axis=0), until // 2 - 1, -1)
    pair_far = pair_code // 2
    return (
        packed // model_blocks, packed % model_blocks,
        pair_far // near_size, pair_far % near_size, (pair_code % 2)[::2], last,
    )


def body(sizes, activations, cotangent, up_tiles, down_tiles, up_rows, up_cols, down_rows, down_cols):
    ur, uc, dr, dc = (v[:, 0] for v in (up_rows, up_cols, down_rows, down_cols))
    model_blocks = sizes[0] * activations.shape[1] // 128
    sort = jax.vmap(functools.partial(tables_of, model_blocks=model_blocks))
    order, far, *pair = sort(jnp.stack([uc, dr]), jnp.stack([ur, dc]))
    tables = (
        order[0], far[0], order[1], far[1], ur, uc, dr, dc,
        *(v[0] for v in pair), *(v[1] for v in pair),
    )
    out, inp, ga_u, ga_d, gb_u, gb_d = run_block(
        sizes, tables, activations, cotangent, up_tiles, down_tiles
    )
    up_grad, down_grad = totals(ga_u, gb_u, ga_d, gb_d)
    return out, inp, up_grad, down_grad


def solution(mesh):
    sizes = (mesh.shape["tensor"], mesh.shape["fsdp"] // 2, mesh.shape["dp"])
    in_specs = (
        P(("dp", "fsdp"), "tensor"),
        P(("dp", "fsdp"), "tensor"),
        P(("fsdp", "tensor"), None, None),
        P(("fsdp", "tensor"), None, None),
        P(None, "tensor"),
        P(None, "tensor"),
        P(None, "tensor"),
        P(None, "tensor"),
    )
    out_specs = (
        P(("dp", "fsdp"), "tensor"),
        P(("dp", "fsdp"), "tensor"),
        P(("fsdp", "tensor"), None, None),
        P(("fsdp", "tensor"), None, None),
    )
    return jax.shard_map(
        functools.partial(body, sizes), mesh=mesh, in_specs=in_specs, out_specs=out_specs,
        check_vma=False,
    )
```

profile of v0, /device:TPU:0, one launch (start us, length us, event | category | flops | bytes accessed | tf_op | source)
XLA Modules:
  0.0 204.4 jit_solution(16411686062893799414)
XLA Ops:
  0.7 0.7 pad_add_fusion.1
  1.4 0.1 fusion.1
  1.5 0.2 convert_reduce_fusion
  1.8 0.1 select_reduce_fusion.3
  1.9 0.2 select_reduce_fusion.1
  2.1 0.7 fusion.7
  2.9 0.2 select_reduce_fusion.2
  3.1 0.2 select_reduce_fusion
  3.3 0.6 slice_bitcast_fusion
  3.9 0.6 fusion.8
  4.5 0.6 fusion.9
  5.1 0.6 slice_reduce_fusion
  5.7 0.2 slice.45
  5.9 0.6 fusion.6
  6.5 0.6 slice_reduce_fusion.1
  7.1 186.8 %block_all.1 = (bf16[128,2048]{1,0:T(8,128)(2,1)}, bf16[128,2048]{1,0:T(8,128)(2,1)}, bf16[64,128,128]{2,1,0:T(8,128)(2,1)}, bf16[64,128,128]{2,1,0:T(8,128)(2,1...) custom-call(s32[256]{0:T(256)} %bitcast.27, s32[256]{0:T(256)} %bitcast.25, s32[256]{0:T(256)} %bitcast.26, ...), custom_call_target="tpu_custom_call" | custom-call | tf_op jit(solution)/shard_map/block_all/pallas_call | solution.py:606
  193.9 0.0 copy-start.1
  193.9 0.0 copy-start
  194.0 8.8 %totals.1 = (f32[64,128,128]{2,1,0:T(8,128)}, f32[64,128,128]{2,1,0:T(8,128)}) custom-call(bf16[64,128,128]{2,1,0:T(8,128)(2,1)} %get-tuple-element.14.ga_u, bf16[1,64,128,128]{3,2,1,0:T(8,128)(2,1)} %get-tuple-element.15.gb_u, bf16[64,128,128]{2,1,0:T(8,128)(2,1)} %get-tuple-element.16.ga_d, bf16[1,64,128,128]{3,2,1,0:T(8,128)(2,1)} %get-tuple-element.17.gb_d), custom_call_target="tpu_custom_call" | custom-call | tf_op jit(solution)/shard_map/totals/pallas_call | solution.py:672
  202.8 0.0 copy-done.1
  202.8 0.8 copy.14
  203.6 0.0 copy-done
  203.6 0.8 copy.15
  (8 shorter events, 0.1 us)
Async XLA Ops:
  193.9 8.8 %copy-start.1 = (bf16[128,2048]{1,0:T(8,128)(2,1)S(1)}, bf16[128,2048]{1,0:T(8,128)(2,1)}, u32[]{:S(2)}) copy-start(bf16[128,2048]{1,0:T(8,128)(2,1)} %get-tuple-element.50) | copy-start | bytes 1572868
  193.9 9.6 %copy-start = (bf16[128,2048]{1,0:T(8,128)(2,1)S(1)}, bf16[128,2048]{1,0:T(8,128)(2,1)}, u32[]{:S(2)}) copy-start(bf16[128,2048]{1,0:T(8,128)(2,1)} %get-tuple-element.51) | copy-start | bytes 1572868
where the time goes:
time: 205 us; the launch traced here: 204 us
  Pallas kernels  196 us (96%)
  local copies, waits for them, and re-layouts  5.39 us (3%)
  other arithmetic  2.65 us (1%)
    pallas_call x1, Pallas kernels, run_block(): pl.pallas_call(functools.partial(block_kernel, sizes), out_shape=[jax.Sha...  187 us
    pallas_call x1, Pallas kernels, totals(): pl.pallas_call(total_kernel, grid=(per // step,), out_shape=[jax.ShapeDty...  8.82 us

commit v1 on v0

--- a/solution.py
+++ b/solution.py
@@ -9,14 +9,15 @@
 
 MESH = pl.DeviceIdType.MESH
 COL_TILES = 8
-PIECES = 16
-CHUNKS = 2
+PIECES = 32
+CHUNKS = 4
 WEIGHT_CHUNKS = 4
-PARTS = 4
+PARTS = 8
+LANES = 128
 
 SHARD_TIME = 11.3
-PIECE_TIME = 2.8
 WEIGHT_TIME = 5.6
+PIECE_SHARE = 2
 
 inv_root_two = 0.7071067811865476
 inv_root_tau = 0.3989422804014327
@@ -76,15 +77,54 @@
     pl.semaphore_wait(barrier, sides + 1 + (chips - 1) + (replicas - 1))
 
 
+def padded(size):
+    return -(-size // LANES) * LANES
+
+
+def tables_of(near, far, model_blocks):
+    count = near.shape[1]
+    near_size = count // COL_TILES + 1
+    spare = (near_size - 1) * 2
+    wide_count = padded(count + model_blocks)
+
+    def along(size, axis, rows=count):
+        return lax.broadcasted_iota(jnp.int32, (rows, size), axis)
+
+    def total(picked, values, axis):
+        return jnp.sum(jnp.where(picked, values, 0), axis=axis, keepdims=True)
+
+    down, over = along(count, 0), along(count, 1)
+    same = down == over
+    before = over < down
+    at = along(1, 0)
+    near_c, far_c = total(same, near, 1), total(same, far, 1)
+    spot = near_c * COL_TILES + total((near == near_c) & before, 1, 1)
+    packed = total(spot == over, at * model_blocks + far_c, 0)
+    equal = far == far_c
+    rank = total(equal & before, 1, 1)
+    often = total(equal, 1, 1)
+    takes = jnp.where((rank == often - 1) & (often % 2 == 1), 2, 1)
+    place_of = rank + total(far < far_c, total(same, takes, 0), 1)
+    code = (at * near_size + near_c) * 2 + jnp.where(rank == 0, 1, 0) - spare
+    pair_code = total(place_of == along(wide_count, 1), code, 0) + spare
+    block = along(padded(model_blocks), 1)
+    until = total(far_c <= block, takes, 0)
+    last = jnp.where(total(far_c == block, 1, 0) > 0, until // 2 - 1, -1)
+    pair_far = pair_code // 2
+    return (
+        packed // model_blocks, packed % model_blocks,
+        pair_far // near_size, pair_far % near_size, pair_code % 2, last,
+    )
+
+
 def block_kernel(
-    sizes, uo, uf, do, df, up_rows, up_cols, down_rows, down_cols,
-    pair_order_u, pair_near_u, pair_first_u, last_u, pair_order_d, pair_near_d, pair_first_d, last_d,
+    sizes, up_rows, up_cols, down_rows, down_cols, ur, uc, dr, dc,
     act, cot, up, down,
     out, inp, ga_u, ga_d, gb_u, gb_d,
     x_all, xt_own, xt_mate, cot_own, cot_mate, u_all, d_all, hidden, ht_own, ht_mate, slope,
-    pg_own, pg_mate, run, acc, parts_o, parts_i, held_r, held_l, stage, x_in,
+    pg_own, pg_mate, run, acc, parts_o, parts_i, held_r, held_l, stage, x_in, made, tables,
     load_sem, zs_sem, zr_sem, ms_sem, mr_sem, ts_sem, tr_sem, ws_sem, wr_sem, ys_sem, yr_sem, cs_sem, cr_sem,
-    os_sem, or_sem, hs_sem, hr_sem, gs_sem, gr_sem, ls_sem, lr_sem, xs_sem, xr_sem, es_sem, er_sem, keep_sem,
+    os_sem, or_sem, hs_sem, hr_sem, gs_sem, gr_sem, ls_sem, lr_sem, xs_sem, xr_sem, es_sem, er_sem, keep_sem, table_sem,
 ):
     n, chips, replicas = sizes
     z, r, c, y = place(sizes)
@@ -254,7 +294,8 @@
         def _(h):
             spots = [h * COL_TILES + k for k in range(COL_TILES)]
             pre = mm(
-                wide([x_all[uf[i]] for i in spots], 1), wide([u_all[uo[i]] for i in spots], 0), 1, 0
+                wide([x_all[tables[0, 1, i]] for i in spots], 1),
+                wide([u_all[tables[0, 0, i]] for i in spots], 0), 1, 0,
             )
             value, tangent = gelu_parts(pre)
             value = value.astype(jnp.bfloat16)
@@ -273,7 +314,8 @@
         def _(h):
             spots = [h * COL_TILES + k for k in range(COL_TILES)]
             value = mm(
-                wide([cot_own[df[i]] for i in spots], 1), wide([d_all[do[i]] for i in spots], 1), 1, 1
+                wide([cot_own[tables[1, 1, i]] for i in spots], 1),
+                wide([d_all[tables[1, 0, i]] for i in spots], 1), 1, 1,
             )
             pg_own[h] = (value * slope[h]).astype(jnp.bfloat16)
 
@@ -285,9 +327,7 @@
     pair_width = 4
 
     def run_part(a, g):
-        order, near, fresh = (
-            (pair_order_d, pair_near_d, pair_first_d) if a == 0 else (pair_order_u, pair_near_u, pair_first_u)
-        )
+        t = 1 - a
         left, right, cut = (hidden, d_all, 0) if a == 0 else (pg_own, u_all, 1)
         steps = run.shape[0] // PARTS // pair_width
         if g == 0:
@@ -298,10 +338,10 @@
             total = acc[...]
             for i in [b * pair_width + k for k in range(pair_width)]:
                 product = mm(
-                    wide([left[near[2 * i]], left[near[2 * i + 1]]], 1),
-                    wide([right[order[2 * i]], right[order[2 * i + 1]]], cut), 1, cut,
+                    wide([left[tables[t, 3, 2 * i]], left[tables[t, 3, 2 * i + 1]]], 1),
+                    wide([right[tables[t, 2, 2 * i]], right[tables[t, 2, 2 * i + 1]]], cut), 1, cut,
                 )
-                total = jnp.where(fresh[i] == 1, 0.0, total) + product
+                total = jnp.where(tables[t, 4, 2 * i] == 1, 0.0, total) + product
                 run[i] = total.astype(jnp.bfloat16)
             acc[...] = total
 
@@ -323,12 +363,11 @@
         return n - 1 - i > z if way > 0 else i < z
 
     def settle(a):
-        last = last_d if a == 0 else last_u
         target = parts[a]
 
         @pl.loop(0, target.shape[0])
         def _(b):
-            spot = last[b]
+            spot = tables[1 - a, 5, b]
             found = run[jnp.maximum(spot, 0)]
             target[b] = jnp.where(spot >= 0, found, jnp.zeros_like(found))
 
@@ -412,8 +451,8 @@
             {"fsdp": q * 2 + c},
         )
 
-    def hand_over(a):
-        @pl.loop(0, pieces)
+    def hand_over(a, first_piece, end):
+        @pl.loop(first_piece, end)
         def _(k):
             for d in range(1, chips):
                 first = first_tile(lax.rem(r + d, chips), k)
@@ -465,12 +504,17 @@
                     w_copy(a, d, k).start()
         for a in range(2):
             own_core(a).start()
-        for k in range(CHUNKS):
-            turn(0, k, 1)
         for copy in loads[1]:
             copy.wait()
         for k in range(CHUNKS):
             mate_chunk(1, 0, k, 1).start()
+        for t, (near, far) in enumerate(((uc, ur), (dr, dc))):
+            for row, values in enumerate(tables_of(near[...], far[...], n * blocks)):
+                made[t, pl.ds(row, 1), pl.ds(0, values.shape[1])] = values
+        pltpu.make_async_copy(made, tables, table_sem).start()
+        for k in range(CHUNKS):
+            turn(0, k, 1)
+        pltpu.make_async_copy(made, tables, table_sem).wait()
 
     at(0.0, start_all)
     chunk_time = SHARD_TIME / CHUNKS
@@ -492,11 +536,11 @@
     at(down_in + 2.0, weights_in, 1)
     hidden_from = max(act_in, up_in + 2.0) + 0.5
     for g in range(PARTS):
-        at(hidden_from + 3.0 * g, hidden_part, g)
-    out_from = max(hidden_from + 3.0 * PARTS, down_in + 2.0) + 0.5
+        at(hidden_from + 1.5 * g, hidden_part, g)
+    out_from = max(hidden_from + 1.5 * PARTS, down_in + 2.0) + 0.5
     for g in range(PARTS):
-        at(out_from + 2.0 * g, run_part, 0, g)
-    out_settle = out_from + 2.0 * PARTS
+        at(out_from + 1.2 * g, run_part, 0, g)
+    out_settle = out_from + 1.2 * PARTS
     at(out_settle, settle, 0)
     for s in range(1, n):
         for k in range(CHUNKS):
@@ -509,23 +553,28 @@
             hidden_mate(g).wait_recv()
 
     at(cot_in, cot_ready)
-    at(cot_in + 0.1, hand_over, 0)
-    slope_from = cot_in + 7.0
+    piece_time = 2 * SHARD_TIME * PIECE_SHARE / pieces
+    group = max(pieces // 8, 1)
+    at(cot_in + 0.1, hand_over, 0, 0, group)
+    for k in range(group, pieces, group):
+        at(cot_in + 0.2 + 1.2 * (k // group), hand_over, 0, k, min(k + group, pieces))
+    slope_from = cot_in + 9.0
     for g in range(PARTS):
-        at(slope_from + 2.5 * g, slope_part, g)
+        at(slope_from + 1.5 * g, slope_part, g)
 
     def grads_ready():
         mate_chunks(0, lambda copy: copy.wait_recv())
         for g in range(PARTS):
             grad_mate(g).wait_recv()
 
-    up_from = slope_from + 2.5 * PARTS
+    up_from = slope_from + 1.5 * PARTS + 1.0
     at(up_from, grads_ready)
-    at(up_from + 0.1, hand_over, 1)
-    inp_from = up_from + 7.0
+    for k in range(0, pieces, group):
+        at(up_from + 0.1 + 1.4 * (k // group), hand_over, 1, k, min(k + group, pieces))
+    inp_from = up_from + 0.1 + 1.4 * 8
     for g in range(PARTS):
-        at(inp_from + 2.0 * g, run_part, 1, g)
-    inp_settle = inp_from + 2.0 * PARTS
+        at(inp_from + 1.5 * g, run_part, 1, g)
+    inp_settle = inp_from + 1.5 * PARTS
     at(inp_settle, settle, 1)
     for a, start in enumerate((out_settle, inp_settle)):
         for t in range(1, n - 1):
@@ -533,7 +582,7 @@
         at(start + 3.0 + (n - 1) * SHARD_TIME, finish, a)
     for a in range(2):
         for k in range(pieces):
-            when = cot_in + 4.0 + PIECE_TIME * (a * pieces + k + 1)
+            when = cot_in + 2.2 + piece_time * (a * pieces + k + 1)
             at(max(when, up_from + 0.2) if a else when, x_event, a, k)
 
     plan.sort(key=lambda item: item[0])
@@ -579,7 +628,7 @@
                 e_copy(a, k, e).wait()
 
 
-def run_block(sizes, tables, activations, cotangent, up_tiles, down_tiles):
+def run_block(sizes, lists, activations, cotangent, up_tiles, down_tiles):
     n, chips, replicas = sizes
     rows, features = activations.shape
     blocks = features // 128
@@ -610,7 +659,7 @@
             + [jax.ShapeDtypeStruct((per, 128, 128), kind)] * 2
             + [jax.ShapeDtypeStruct((replicas - 1, per, 128, 128), kind)] * 2
         ),
-        in_specs=[smem] * len(tables) + [anywhere] * 4,
+        in_specs=[smem] * 4 + [vmem] * 4 + [anywhere] * 4,
         out_specs=[vmem] * 2 + [anywhere] * 4,
         scratch_shapes=[
             held(model_blocks),
@@ -634,6 +683,8 @@
             held(2, n - 1, blocks),
             pltpu.VMEM((2, chips - 1, per, 128, 128), kind),
             pltpu.VMEM((2, chips - 1, per, 128, 128), kind),
+            pltpu.VMEM((2, 8, padded(total_tiles + model_blocks)), jnp.int32),
+            pltpu.SMEM((2, 8, padded(total_tiles + model_blocks)), jnp.int32),
             dma((4, blocks)),
             *twice(2, 2, n, CHUNKS),
             *twice(2, n, CHUNKS),
@@ -648,12 +699,13 @@
             *twice(2, pieces, chips),
             *twice(2, pieces, replicas),
             dma((2, pieces)),
+            dma,
         ],
         compiler_params=pltpu.CompilerParams(
             collective_id=0, has_side_effects=True, vmem_limit_bytes=67043328
         ),
         name="block_all",
-    )(*tables, activations, cotangent, up_tiles, down_tiles)
+    )(*(v[:, 0] for v in lists), *(v.T for v in lists), activations, cotangent, up_tiles, down_tiles)
 
 
 def total_kernel(ga_u, gb_u, ga_d, gb_d, up_grad, down_grad):
@@ -666,7 +718,7 @@
 
 def totals(ga_u, gb_u, ga_d, gb_d):
     per = ga_u.shape[0]
-    step = min(8, per)
+    step = max(per // 2, 1)
     one = pl.BlockSpec((step, 128, 128), lambda i: (i, 0, 0))
     more = pl.BlockSpec((gb_u.shape[0], step, 128, 128), lambda i: (0, i, 0, 0))
     return pl.pallas_call(
@@ -679,44 +731,10 @@
     )(ga_u, gb_u, ga_d, gb_d)
 
 
-def tables_of(near, far, model_blocks):
-    count = near.shape[0]
-    near_size = count // COL_TILES + 1
-    at = lax.iota(jnp.int32, count)
-    before = at[:, None] < at[None, :]
-    equal = far[:, None] == far[None, :]
-    spot = near * COL_TILES + jnp.sum(((near[:, None] == near[None, :]) & before).astype(jnp.int32), axis=0)
-    here = spot[:, None] == at[None, :]
-    packed = jnp.sum(jnp.where(here, (at * model_blocks + far)[:, None], 0), axis=0)
-    rank = jnp.sum((equal & before).astype(jnp.int32), axis=0)
-    often = jnp.sum(equal.astype(jnp.int32), axis=0)
-    takes = 1 + jnp.where((rank == often - 1) & (often % 2 == 1), 1, 0)
-    place_of = rank + jnp.sum(jnp.where(far[:, None] < far[None, :], takes[:, None], 0), axis=0)
-    there = place_of[:, None] == lax.iota(jnp.int32, count + model_blocks)[None, :]
-    code = ((at * near_size + near) * 2 + (rank == 0)) - (near_size - 1) * 2
-    pair_code = jnp.sum(jnp.where(there, code[:, None], 0), axis=0) + (near_size - 1) * 2
-    block = lax.iota(jnp.int32, model_blocks)
-    matches = far[:, None] == block[None, :]
-    until = jnp.sum(jnp.where(far[:, None] <= block[None, :], takes[:, None], 0), axis=0)
-    last = jnp.where(jnp.any(matches, axis=0), until // 2 - 1, -1)
-    pair_far = pair_code // 2
-    return (
-        packed // model_blocks, packed % model_blocks,
-        pair_far // near_size, pair_far % near_size, (pair_code % 2)[::2], last,
-    )
-
-
 def body(sizes, activations, cotangent, up_tiles, down_tiles, up_rows, up_cols, down_rows, down_cols):
-    ur, uc, dr, dc = (v[:, 0] for v in (up_rows, up_cols, down_rows, down_cols))
-    model_blocks = sizes[0] * activations.shape[1] // 128
-    sort = jax.vmap(functools.partial(tables_of, model_blocks=model_blocks))
-    order, far, *pair = sort(jnp.stack([uc, dr]), jnp.stack([ur, dc]))
-    tables = (
-        order[0], far[0], order[1], far[1], ur, uc, dr, dc,
-        *(v[0] for v in pair), *(v[1] for v in pair),
-    )
+    lists = (up_rows, up_cols, down_rows, down_cols)
     out, inp, ga_u, ga_d, gb_u, gb_d = run_block(
-        sizes, tables, activations, cotangent, up_tiles, down_tiles
+        sizes, lists, activations, cotangent, up_tiles, down_tiles
     )
     up_grad, down_grad = totals(ga_u, gb_u, ga_d, gb_d)
     return out, inp, up_grad, down_grad

time: 205 us -> 193 us (0.941)
  Pallas kernels: 196 us -> 191 us
  local copies, waits for them, and re-layouts: 5.39 us -> 1.59 us
  other arithmetic: 2.65 us -> 0 us
    slice x6 -> x0, local copies, waits for them, and re-layouts: 3.2 us -> none  [the longest x3 1.78 us: body(): v[1]]
    pallas_call x1, Pallas kernels: 8.82 us -> 5.94 us  [totals(): pl.pallas_call(total_kernel, grid=(per // step,), out_shape=[jax.ShapeDty...]
where the time goes in v1:
time: 193 us
  Pallas kernels  191 us (99%)
    pallas_call x1, Pallas kernels, run_block(): pl.pallas_call(functools.partial(block_kernel, sizes), out_shape=[jax.Sha...  185 us
    pallas_call x1, Pallas kernels, totals(): pl.pallas_call(total_kernel, grid=(per // step,), out_shape=[jax.ShapeDty...  5.94 us

profile of v1, /device:TPU:0, one launch (start us, length us, event | category | flops | bytes accessed | tf_op | source)
XLA Modules:
  0.0 193.3 jit_solution(9010634966805289374)
XLA Ops:
  0.6 185.1 %block_all.1 = (bf16[128,2048]{1,0:T(8,128)(2,1)}, bf16[128,2048]{1,0:T(8,128)(2,1)}, bf16[64,128,128]{2,1,0:T(8,128)(2,1)}, bf16[64,128,128]{2,1,0:T(8,128)(2,1...) custom-call(s32[256]{0:T(256)} %bitcast.8, s32[256]{0:T(256)} %bitcast.10, s32[256]{0:T(256)} %bitcast.12, ...), custom_call_target="tpu_custom_call" | custom-call | tf_op jit(solution)/shard_map/block_all/pallas_call | solution.py:655
  185.8 0.0 copy-start.1
  185.8 0.0 copy-start
  185.8 5.9 %totals.1 = (f32[64,128,128]{2,1,0:T(8,128)}, f32[64,128,128]{2,1,0:T(8,128)}) custom-call(bf16[64,128,128]{2,1,0:T(8,128)(2,1)} %get-tuple-element.14.ga_u, bf16[1,64,128,128]{3,2,1,0:T(8,128)(2,1)} %get-tuple-element.15.gb_u, bf16[64,128,128]{2,1,0:T(8,128)(2,1)} %get-tuple-element.16.ga_d, bf16[1,64,128,128]{3,2,1,0:T(8,128)(2,1)} %get-tuple-element.17.gb_d), custom_call_target="tpu_custom_call" | custom-call | tf_op jit(solution)/shard_map/totals/pallas_call | solution.py:724
  191.7 0.0 copy-done.1
  191.7 0.8 copy.14
  192.5 0.0 copy-done
  192.5 0.8 copy.15
Async XLA Ops:
  185.8 6.0 %copy-start.1 = (bf16[128,2048]{1,0:T(8,128)(2,1)S(1)}, bf16[128,2048]{1,0:T(8,128)(2,1)}, u32[]{:S(2)}) copy-start(bf16[128,2048]{1,0:T(8,128)(2,1)} %get-tuple-element.24) | copy-start | bytes 1572868
  185.8 6.8 %copy-start = (bf16[128,2048]{1,0:T(8,128)(2,1)S(1)}, bf16[128,2048]{1,0:T(8,128)(2,1)}, u32[]{:S(2)}) copy-start(bf16[128,2048]{1,0:T(8,128)(2,1)} %get-tuple-element.25) | copy-start | bytes 1572868

commit v2 on v1

--- a/solution.py
+++ b/solution.py
@@ -13,6 +13,7 @@
 CHUNKS = 4
 WEIGHT_CHUNKS = 4
 PARTS = 8
+HIDDEN_PARTS = 4
 LANES = 128
 
 SHARD_TIME = 11.3
@@ -87,29 +88,35 @@
     spare = (near_size - 1) * 2
     wide_count = padded(count + model_blocks)
 
-    def along(size, axis, rows=count):
-        return lax.broadcasted_iota(jnp.int32, (rows, size), axis)
-
-    def total(picked, values, axis):
-        return jnp.sum(jnp.where(picked, values, 0), axis=axis, keepdims=True)
-
-    down, over = along(count, 0), along(count, 1)
-    same = down == over
-    before = over < down
-    at = along(1, 0)
-    near_c, far_c = total(same, near, 1), total(same, far, 1)
-    spot = near_c * COL_TILES + total((near == near_c) & before, 1, 1)
-    packed = total(spot == over, at * model_blocks + far_c, 0)
-    equal = far == far_c
-    rank = total(equal & before, 1, 1)
-    often = total(equal, 1, 1)
+    def along(size, axis):
+        return lax.broadcasted_iota(jnp.int32, (count, size), axis)
+
+    def column(row, size):
+        turned = jnp.broadcast_to(row, (LANES, count)).T
+        return wide([turned] * (size // LANES), 1)
+
+    def total(picked, values):
+        return jnp.sum(jnp.where(picked, values, 0), axis=0, keepdims=True)
+
+    at, over, over_wide = along(count, 0), along(count, 1), along(wide_count, 1)
+    before = at < over
+    near_c, far_c = column(near, wide_count), column(far, wide_count)
+    near_n, far_n = near_c[:, :count], far_c[:, :count]
+    spot = near * COL_TILES + total((near_n == near) & before, 1)
+    packed = total(column(spot, count) == over, at * model_blocks + far_n)
+    equal = far_n == far
+    rank = total(equal & before, 1)
+    often = total(equal, 1)
     takes = jnp.where((rank == often - 1) & (often % 2 == 1), 2, 1)
-    place_of = rank + total(far < far_c, total(same, takes, 0), 1)
-    code = (at * near_size + near_c) * 2 + jnp.where(rank == 0, 1, 0) - spare
-    pair_code = total(place_of == along(wide_count, 1), code, 0) + spare
-    block = along(padded(model_blocks), 1)
-    until = total(far_c <= block, takes, 0)
-    last = jnp.where(total(far_c == block, 1, 0) > 0, until // 2 - 1, -1)
+    takes_c = column(takes, count)
+    place_of = rank + total(far_n < far, takes_c)
+    place_c = column(place_of * 2 + jnp.where(rank == 0, 1, 0), wide_count)
+    code = (along(wide_count, 0) * near_size + near_c) * 2 + place_c % 2 - spare
+    pair_code = total(place_c // 2 == over_wide, code) + spare
+    ends = padded(model_blocks)
+    block = along(ends, 1)
+    until = total(far_c[:, :ends] <= block, takes_c[:, :ends])
+    last = jnp.where(total(far_c[:, :ends] == block, 1) > 0, until // 2 - 1, -1)
     pair_far = pair_code // 2
     return (
         packed // model_blocks, packed % model_blocks,
@@ -140,27 +147,31 @@
     pieces = min(PIECES, per)
     size = per // pieces
     span = hidden_blocks // PARTS
+    hidden_span = hidden_blocks // HIDDEN_PARTS
     features = (x_all, cot_own)
     weights = ((up, u_all), (down, d_all))
     mate = {"fsdp": r * 2 + 1 - c}
 
-    loads = ([], [])
+    loads = []
     for a, (src, full) in enumerate(((act, x_all), (cot, cot_own))):
         for b in range(blocks):
-            copy = pltpu.make_async_copy(
-                src.at[:, pl.ds(b * 128, 128)], full.at[z * blocks + b], load_sem.at[a, b]
-            )
-            copy.start()
-            loads[a].append(copy)
+            pltpu.make_async_copy(
+                src.at[:, pl.ds(b * 128, 128)], full.at[z * blocks + b], load_sem.at[a]
+            ).start()
+        own = full.at[pl.ds(z * blocks, blocks)]
+        loads.append(pltpu.make_async_copy(own, own, load_sem.at[a]))
     weight_loads = []
     for a, (src, full) in enumerate(weights):
-        copy = pltpu.make_async_copy(src, full.at[pl.ds(f * per, per)], load_sem.at[2 + a, 0])
+        copy = pltpu.make_async_copy(src, full.at[pl.ds(f * per, per)], load_sem.at[2 + a])
         copy.start()
         weight_loads.append(copy)
     hidden[hidden_blocks] = jnp.zeros(hidden.shape[1:], hidden.dtype)
     pg_own[hidden_blocks] = jnp.zeros(pg_own.shape[1:], pg_own.dtype)
     enter(sizes)
 
+    def part_shard(ref, s):
+        return ref.at[pl.ds(s * blocks, blocks)]
+
     def shard(full, s, k):
         return full.at[pl.ds(s * blocks + k * chunk, chunk)]
 
@@ -168,8 +179,15 @@
         piece = shard(features[a], z - way * s, k)
         w = 0 if way > 0 else 1
         return remote(
-            piece, piece, zs_sem.at[a, w, s, k], zr_sem.at[a, w, s, k], {"tensor": z + way}
+            piece, piece, zs_sem.at[a, w, s], zr_sem.at[a, w, s, k], {"tensor": z + way}
         )
+
+    def line_sent(a, s, way):
+        whole = part_shard(features[a], z - way * s)
+        w = 0 if way > 0 else 1
+        remote(
+            whole, whole, zs_sem.at[a, w, s], zr_sem.at[a, w, s, 0], {"tensor": z + way}
+        ).wait_send()
 
     def can_send(way):
         return z < n - 1 if way > 0 else z > 0
@@ -185,23 +203,27 @@
                 def _():
                     line(a, 0, k, way).start()
 
-    def mate_chunk(a, s, k, way):
+    def mate_copy(src, dst, s, way):
         w = 0 if way > 0 else 1
-        src, dst = ((xt_own, xt_mate), (cot_own, cot_mate))[a]
-        sems = ((ts_sem, tr_sem), (ms_sem, mr_sem))[a]
-        return remote(
-            shard(src, z - way * s, k), shard(dst, z - way * s, k),
-            sems[0].at[w, s, k], sems[1].at[w, s, k], mate,
-        )
-
-    def turn(s, k, way):
-        first = (z - way * s) * blocks + k * chunk
-
-        @pl.loop(0, chunk)
+        return remote(src, dst, ms_sem.at[w, s], mr_sem.at[w, s], mate)
+
+    def mate_chunk(s, k, way):
+        return mate_copy(shard(cot_own, z - way * s, k), shard(cot_mate, z - way * s, k), s, way)
+
+    def mate_turned(s, way):
+        w = 0 if way > 0 else 1
+        at = pl.ds((z - way * s) * blocks, blocks)
+        return remote(xt_own.at[at], xt_mate.at[at], ts_sem.at[w, s], tr_sem.at[w, s], mate)
+
+    def turn(s, way):
+        first = (z - way * s) * blocks
+
+        @pl.loop(0, blocks // 2)
         def _(b):
-            xt_own[first + b] = x_all[first + b].T
-
-        mate_chunk(0, s, k, way).start()
+            for i in range(2):
+                xt_own[first + 2 * b + i] = x_all[first + 2 * b + i].T
+
+        mate_turned(s, way).start()
 
     def z_event(a, s, k):
         for way in (1, -1):
@@ -216,24 +238,32 @@
                         line(a, s, k, way).start()
 
                 if a == 1:
-                    mate_chunk(1, s, k, way).start()
-
-    def turn_event(s, k):
+                    mate_chunk(s, k, way).start()
+
+    def turn_event(s):
         for way in (1, -1):
 
             @pl.when(has(s, way))
             def _():
-                turn(s, k, way)
-
-    def mate_chunks(a, act_on):
-        for k in range(CHUNKS):
-            act_on(mate_chunk(a, 0, k, 1))
-            for s in range(1, n):
-                for way in (1, -1):
-
-                    @pl.when(has(s, way))
-                    def _():
-                        act_on(mate_chunk(a, s, k, way))
+                turn(s, way)
+
+    def mate_chunks(act_on):
+        def each(s, way):
+            act_on(mate_copy(part_shard(cot_own, z - way * s), part_shard(cot_mate, z - way * s), s, way))
+
+        each(0, 1)
+        for s in range(1, n):
+            for way in (1, -1):
+                pl.when(has(s, way))(functools.partial(each, s, way))
+
+    def mate_turns(act_on):
+        act_on(mate_turned(0, 1))
+        for s in range(1, n):
+            for way in (1, -1):
+
+                @pl.when(has(s, way))
+                def _():
+                    act_on(mate_turned(s, way))
 
     def tile_range(full, r_of, q, k):
         return full.at[pl.ds((r_of * 2 + c) * per + q * part + k * weight_size, weight_size)]
@@ -244,20 +274,43 @@
     def w_copy(a, d, k):
         src = weights[a][0].at[pl.ds(y * part + k * weight_size, weight_size)]
         return remote(
-            src, tile_range(weights[a][1], r, y, k), ws_sem.at[a, d, k], wr_sem.at[a, d, k],
+            src, tile_range(weights[a][1], r, y, k), ws_sem.at[a, d - 1], wr_sem.at[a, d - 1, k],
             {"fsdp": lax.rem(r + d, chips) * 2 + c},
         )
 
     def y_copy(a, d, e, k):
         piece = tile_range(weights[a][1], from_chip(d), y, k)
         return remote(
-            piece, piece, ys_sem.at[a, d, e, k], yr_sem.at[a, d, e, k],
+            piece, piece, ys_sem.at[a, d - 1, e - 1], yr_sem.at[a, d - 1, e - 1, k],
             {"dp": lax.rem(y + e, replicas)},
         )
 
     def core_copy(a, d, e, k):
         piece = tile_range(weights[a][1], from_chip(d), lax.rem(y - e + replicas, replicas), k)
-        return remote(piece, piece, cs_sem.at[a, d, e, k], cr_sem.at[a, d, e, k], mate)
+        return remote(piece, piece, cs_sem.at[a, d - 1, e], cr_sem.at[a, d - 1, e], mate)
+
+    def share(full, r_of, q):
+        return full.at[pl.ds((r_of * 2 + c) * per + q * part, part)]
+
+    def core_copies(a, d, e):
+        whole = share(weights[a][1], from_chip(d), lax.rem(y - e + replicas, replicas))
+        return remote(whole, whole, cs_sem.at[a, d - 1, e], cr_sem.at[a, d - 1, e], mate)
+
+    def weights_sent(a):
+        own_core(a).wait_send()
+        for d in range(1, chips):
+            remote(
+                weights[a][0].at[pl.ds(y * part, part)], share(weights[a][1], r, y),
+                ws_sem.at[a, d - 1], wr_sem.at[a, d - 1, 0], {"fsdp": lax.rem(r + d, chips) * 2 + c},
+            ).wait_send()
+            for e in range(replicas):
+                core_copies(a, d, e).wait_send()
+            for e in range(1, replicas):
+                whole = share(weights[a][1], from_chip(d), y)
+                remote(
+                    whole, whole, ys_sem.at[a, d - 1, e - 1], yr_sem.at[a, d - 1, e - 1, 0],
+                    {"dp": lax.rem(y + e, replicas)},
+                ).wait_send()
 
     def own_core(a):
         return remote(
@@ -282,15 +335,17 @@
         own_core(a).wait_recv()
         for d in range(1, chips):
             for e in range(replicas):
-                for k in range(weight_chunks):
-                    core_copy(a, d, e, k).wait_recv()
+                core_copies(a, d, e).wait_recv()
 
     def hidden_mate(g):
-        at = pl.ds(g * span, span)
-        return remote(ht_own.at[at], ht_mate.at[at], hs_sem.at[g], hr_sem.at[g], mate)
+        at = pl.ds(g * hidden_span, hidden_span)
+        return remote(ht_own.at[at], ht_mate.at[at], hs_sem.at[0], hr_sem.at[0], mate)
+
+    def hidden_mates():
+        return remote(ht_own, ht_mate, hs_sem.at[0], hr_sem.at[0], mate)
 
     def hidden_part(g):
-        @pl.loop(g * span, (g + 1) * span)
+        @pl.loop(g * hidden_span, (g + 1) * hidden_span)
         def _(h):
             spots = [h * COL_TILES + k for k in range(COL_TILES)]
             pre = mm(
@@ -307,7 +362,11 @@
 
     def grad_mate(g):
         at = pl.ds(g * span, span)
-        return remote(pg_own.at[at], pg_mate.at[at], gs_sem.at[g], gr_sem.at[g], mate)
+        return remote(pg_own.at[at], pg_mate.at[at], gs_sem.at[0], gr_sem.at[0], mate)
+
+    def grad_mates():
+        at = pl.ds(0, hidden_blocks)
+        return remote(pg_own.at[at], pg_mate, gs_sem.at[0], gr_sem.at[0], mate)
 
     def slope_part(g):
         @pl.loop(g * span, (g + 1) * span)
@@ -326,10 +385,12 @@
     held = (held_r, held_l)
     pair_width = 4
 
+    run_parts = (HIDDEN_PARTS, PARTS)
+
     def run_part(a, g):
         t = 1 - a
         left, right, cut = (hidden, d_all, 0) if a == 0 else (pg_own, u_all, 1)
-        steps = run.shape[0] // PARTS // pair_width
+        steps = run.shape[0] // run_parts[a] // pair_width
         if g == 0:
             acc[...] = jnp.zeros_like(acc)
 
@@ -345,9 +406,6 @@
                 run[i] = total.astype(jnp.bfloat16)
             acc[...] = total
 
-    def part_shard(ref, s):
-        return ref.at[pl.ds(s * blocks, blocks)]
-
     def fold(a, i, way, source):
         s = n - 1 - i if way > 0 else i
         k = 0 if way > 0 else 1
@@ -447,7 +505,7 @@
         q = lax.rem(r + d, chips)
         at = pl.ds(k * size, size)
         return remote(
-            stage.at[a, d - 1, at], x_in.at[a, d - 1, at], xs_sem.at[a, k, d], xr_sem.at[a, k, d],
+            stage.at[a, d - 1, at], x_in.at[a, d - 1, at], xs_sem.at[a, d - 1], xr_sem.at[a, k, d - 1],
             {"fsdp": q * 2 + c},
         )
 
@@ -467,13 +525,16 @@
     def e_copy(a, k, e):
         return remote(
             done_piece(a, k), others[a].at[e - 1, pl.ds(k * size, size)],
-            es_sem.at[a, k, e], er_sem.at[a, k, e], {"dp": lax.rem(y + e, replicas)},
+            es_sem.at[a, e - 1], er_sem.at[a, e - 1], {"dp": lax.rem(y + e, replicas)},
         )
 
     def keep_copy(a, k):
         return pltpu.make_async_copy(
-            done_piece(a, k), sums[a].at[pl.ds(k * size, size)], keep_sem.at[a, k]
+            done_piece(a, k), sums[a].at[pl.ds(k * size, size)], keep_sem.at[a]
         )
+
+    def x_events(a, first_piece, end):
+        pl.loop(first_piece, end)(functools.partial(x_event, a))
 
     def x_event(a, k):
         first = first_tile(r, k)
@@ -495,8 +556,7 @@
         plan.append((time, functools.partial(work, *args)))
 
     def start_all():
-        for copy in loads[0]:
-            copy.wait()
+        loads[0].wait()
         z_start(0)
         for a in range(2):
             for k in range(weight_chunks):
@@ -504,25 +564,30 @@
                     w_copy(a, d, k).start()
         for a in range(2):
             own_core(a).start()
-        for copy in loads[1]:
-            copy.wait()
+        loads[1].wait()
         for k in range(CHUNKS):
-            mate_chunk(1, 0, k, 1).start()
-        for t, (near, far) in enumerate(((uc, ur), (dr, dc))):
-            for row, values in enumerate(tables_of(near[...], far[...], n * blocks)):
-                made[t, pl.ds(row, 1), pl.ds(0, values.shape[1])] = values
-        pltpu.make_async_copy(made, tables, table_sem).start()
-        for k in range(CHUNKS):
-            turn(0, k, 1)
-        pltpu.make_async_copy(made, tables, table_sem).wait()
+            mate_chunk(0, k, 1).start()
+
+    def table_copy(t):
+        return pltpu.make_async_copy(made.at[t], tables.at[t], table_sem.at[t])
+
+    def make_table(t):
+        near, far = ((uc, ur), (dr, dc))[t]
+        for row, values in enumerate(tables_of(near[...], far[...], n * blocks)):
+            made[t, pl.ds(row, 1), pl.ds(0, values.shape[1])] = values
+        table_copy(t).start()
 
     at(0.0, start_all)
+    for t in range(2):
+        at(10.2 + 5.65 * t, make_table, t)
+        at(24.0, lambda t: table_copy(t).wait(), t)
+    at(5.7, turn, 0, 1)
     chunk_time = SHARD_TIME / CHUNKS
     for s in range(1, n):
         for k in range(CHUNKS):
             when = 2.0 + ((s - 1) * CHUNKS + k + 1) * chunk_time
             at(when, z_event, 0, s, k)
-            at(when + 0.1, turn_event, s, k)
+        at(2.0 + s * SHARD_TIME + 0.1 + chunk_time, turn_event, s)
     act_in = 2.0 + (n - 1) * SHARD_TIME
     at(2.05 + max(n - 2, 0) * SHARD_TIME, z_start, 1)
     for a in range(2):
@@ -535,12 +600,12 @@
     at(up_in + 2.0, weights_in, 0)
     at(down_in + 2.0, weights_in, 1)
     hidden_from = max(act_in, up_in + 2.0) + 0.5
-    for g in range(PARTS):
-        at(hidden_from + 1.5 * g, hidden_part, g)
-    out_from = max(hidden_from + 1.5 * PARTS, down_in + 2.0) + 0.5
-    for g in range(PARTS):
-        at(out_from + 1.2 * g, run_part, 0, g)
-    out_settle = out_from + 1.2 * PARTS
+    for g in range(HIDDEN_PARTS):
+        at(hidden_from + 3.0 * g, hidden_part, g)
+    out_from = max(hidden_from + 3.0 * HIDDEN_PARTS, down_in + 2.0) + 0.5
+    for g in range(HIDDEN_PARTS):
+        at(out_from + 2.4 * g, run_part, 0, g)
+    out_settle = out_from + 2.4 * HIDDEN_PARTS
     at(out_settle, settle, 0)
     for s in range(1, n):
         for k in range(CHUNKS):
@@ -548,9 +613,8 @@
     cot_in = max(act_in + (n - 1) * SHARD_TIME, out_settle) + 1.0
 
     def cot_ready():
-        mate_chunks(1, lambda copy: copy.wait_recv())
-        for g in range(PARTS):
-            hidden_mate(g).wait_recv()
+        mate_chunks(lambda copy: copy.wait_recv())
+        hidden_mates().wait_recv()
 
     at(cot_in, cot_ready)
     piece_time = 2 * SHARD_TIME * PIECE_SHARE / pieces
@@ -563,9 +627,8 @@
         at(slope_from + 1.5 * g, slope_part, g)
 
     def grads_ready():
-        mate_chunks(0, lambda copy: copy.wait_recv())
-        for g in range(PARTS):
-            grad_mate(g).wait_recv()
+        mate_turns(lambda copy: copy.wait_recv())
+        grad_mates().wait_recv()
 
     up_from = slope_from + 1.5 * PARTS + 1.0
     at(up_from, grads_ready)
@@ -586,26 +649,28 @@
             at(max(when, up_from + 0.2) if a else when, x_event, a, k)
 
     plan.sort(key=lambda item: item[0])
+    steps = []
     for _, work in plan:
+        if work.func is x_event:
+            a, k = work.args
+            if steps and steps[-1].func is x_events and steps[-1].args[::2] == (a, k):
+                work = functools.partial(x_events, a, steps.pop().args[1], k + 1)
+            else:
+                work = functools.partial(x_events, a, k, k + 1)
+        steps.append(work)
+    for work in steps:
         work()
 
+    mate_chunks(lambda copy: copy.wait_send())
+    mate_turns(lambda copy: copy.wait_send())
     for a in range(2):
-        mate_chunks(a, lambda copy: copy.wait_send())
-        own_core(a).wait_send()
-        for d in range(1, chips):
-            for k in range(weight_chunks):
-                w_copy(a, d, k).wait_send()
-                for e in range(replicas):
-                    core_copy(a, d, e, k).wait_send()
-                for e in range(1, replicas):
-                    y_copy(a, d, e, k).wait_send()
+        weights_sent(a)
         for way in (1, -1):
             for s in range(n - 1):
 
                 @pl.when(jnp.logical_and(can_send(way), has(s, way)))
                 def _():
-                    for k in range(CHUNKS):
-                        line(a, s, k, way).wait_send()
+                    line_sent(a, s, way)
 
         for i in range(n - 1):
             for way in (1, -1):
@@ -614,18 +679,20 @@
                 def _():
                     fold(a, i, way, False).wait_send()
 
-    for g in range(PARTS):
-        hidden_mate(g).wait_send()
-        grad_mate(g).wait_send()
+    hidden_mates().wait_send()
+    grad_mates().wait_send()
     for a in range(2):
-
-        @pl.loop(0, pieces)
-        def _(k):
-            for d in range(1, chips):
-                x_copy(a, k, d).wait_send()
-            keep_copy(a, k).wait()
-            for e in range(1, replicas):
-                e_copy(a, k, e).wait()
+        for d in range(1, chips):
+            remote(
+                stage.at[a, d - 1], x_in.at[a, d - 1], xs_sem.at[a, d - 1], xr_sem.at[a, 0, d - 1],
+                {"fsdp": lax.rem(r + d, chips) * 2 + c},
+            ).wait_send()
+        pltpu.make_async_copy(x_in.at[a, 0], sums[a], keep_sem.at[a]).wait()
+        for e in range(1, replicas):
+            remote(
+                x_in.at[a, 0], others[a].at[e - 1], es_sem.at[a, e - 1], er_sem.at[a, e - 1],
+                {"dp": lax.rem(y + e, replicas)},
+            ).wait()
 
 
 def run_block(sizes, lists, activations, cotangent, up_tiles, down_tiles):
@@ -685,21 +752,25 @@
             pltpu.VMEM((2, chips - 1, per, 128, 128), kind),
             pltpu.VMEM((2, 8, padded(total_tiles + model_blocks)), jnp.int32),
             pltpu.SMEM((2, 8, padded(total_tiles + model_blocks)), jnp.int32),
-            dma((4, blocks)),
-            *twice(2, 2, n, CHUNKS),
-            *twice(2, n, CHUNKS),
-            *twice(2, n, CHUNKS),
-            *twice(2, chips, weight_chunks),
-            *twice(2, chips, replicas, weight_chunks),
-            *twice(2, chips, replicas, weight_chunks),
+            dma((4,)),
+            dma((2, 2, n - 1)),
+            dma((2, 2, n - 1, CHUNKS)),
+            *twice(2, n),
+            *twice(2, n),
+            dma((2, chips - 1)),
+            dma((2, chips - 1, weight_chunks)),
+            dma((2, chips - 1, replicas - 1)),
+            dma((2, chips - 1, replicas - 1, weight_chunks)),
+            *twice(2, chips - 1, replicas),
             *twice(2),
-            *twice(PARTS),
-            *twice(PARTS),
-            *twice(2, 2, n),
-            *twice(2, pieces, chips),
-            *twice(2, pieces, replicas),
-            dma((2, pieces)),
-            dma,
+            *twice(1),
+            *twice(1),
+            *twice(2, 2, n - 1),
+            dma((2, chips - 1)),
+            dma((2, pieces, chips - 1)),
+            *twice(2, replicas - 1),
+            dma((2,)),
+            dma((2,)),
         ],
         compiler_params=pltpu.CompilerParams(
             collective_id=0, has_side_effects=True, vmem_limit_bytes=67043328

time: 193 us -> 185 us (0.959)
  Pallas kernels: 191 us -> 183 us
    pallas_call x1, Pallas kernels: 185 us -> 177 us  [run_block(): pl.pallas_call(functools.partial(block_kernel, sizes), out_shape=[jax.Sha...]
where the time goes in v2:
time: 185 us
  Pallas kernels  183 us (99%)
    pallas_call x1, Pallas kernels, run_block(): pl.pallas_call(functools.partial(block_kernel, sizes), out_shape=[jax.Sha...  177 us
    pallas_call x1, Pallas kernels, totals(): pl.pallas_call(total_kernel, grid=(per // step,), out_shape=[jax.ShapeDty...  5.94 us

profile of v2, /device:TPU:0, one launch (start us, length us, event | category | flops | bytes accessed | tf_op | source)
XLA Modules:
  0.0 185.0 jit_solution(6959564450852751107)
XLA Ops:
  0.6 176.8 %block_all.1 = (bf16[128,2048]{1,0:T(8,128)(2,1)}, bf16[128,2048]{1,0:T(8,128)(2,1)}, bf16[64,128,128]{2,1,0:T(8,128)(2,1)}, bf16[64,128,128]{2,1,0:T(8,128)(2,1...) custom-call(s32[256]{0:T(256)} %bitcast.8, s32[256]{0:T(256)} %bitcast.10, s32[256]{0:T(256)} %bitcast.12, ...), custom_call_target="tpu_custom_call" | custom-call | tf_op jit(solution)/shard_map/block_all/pallas_call | solution.py:722
  177.5 0.0 copy-start.1
  177.5 0.0 copy-start
  177.5 5.9 %totals.1 = (f32[64,128,128]{2,1,0:T(8,128)}, f32[64,128,128]{2,1,0:T(8,128)}) custom-call(bf16[64,128,128]{2,1,0:T(8,128)(2,1)} %get-tuple-element.14.ga_u, bf16[1,64,128,128]{3,2,1,0:T(8,128)(2,1)} %get-tuple-element.15.gb_u, bf16[64,128,128]{2,1,0:T(8,128)(2,1)} %get-tuple-element.16.ga_d, bf16[1,64,128,128]{3,2,1,0:T(8,128)(2,1)} %get-tuple-element.17.gb_d), custom_call_target="tpu_custom_call" | custom-call | tf_op jit(solution)/shard_map/totals/pallas_call | solution.py:795
  183.4 0.0 copy-done.1
  183.4 0.8 copy.14
  184.2 0.0 copy-done
  184.2 0.8 copy.15
Async XLA Ops:
  177.5 6.0 %copy-start.1 = (bf16[128,2048]{1,0:T(8,128)(2,1)S(1)}, bf16[128,2048]{1,0:T(8,128)(2,1)}, u32[]{:S(2)}) copy-start(bf16[128,2048]{1,0:T(8,128)(2,1)} %get-tuple-element.24) | copy-start | bytes 1572868
  177.5 6.8 %copy-start = (bf16[128,2048]{1,0:T(8,128)(2,1)S(1)}, bf16[128,2048]{1,0:T(8,128)(2,1)}, u32[]{:S(2)}) copy-start(bf16[128,2048]{1,0:T(8,128)(2,1)} %get-tuple-element.25) | copy-start | bytes 1572868

commit v3 on v2

--- a/solution.py
+++ b/solution.py
@@ -9,8 +9,8 @@
 
 MESH = pl.DeviceIdType.MESH
 COL_TILES = 8
-PIECES = 32
-CHUNKS = 4
+PIECES = 16
+CHUNKS = 2
 WEIGHT_CHUNKS = 4
 PARTS = 8
 HIDDEN_PARTS = 4
@@ -128,10 +128,10 @@
     sizes, up_rows, up_cols, down_rows, down_cols, ur, uc, dr, dc,
     act, cot, up, down,
     out, inp, ga_u, ga_d, gb_u, gb_d,
-    x_all, xt_own, xt_mate, cot_own, cot_mate, u_all, d_all, hidden, ht_own, ht_mate, slope,
+    x_all, flat_o, flat_i, xt_own, xt_mate, cot_own, cot_mate, u_all, d_all, hidden, ht_own, ht_mate, slope,
     pg_own, pg_mate, run, acc, parts_o, parts_i, held_r, held_l, stage, x_in, made, tables,
     load_sem, zs_sem, zr_sem, ms_sem, mr_sem, ts_sem, tr_sem, ws_sem, wr_sem, ys_sem, yr_sem, cs_sem, cr_sem,
-    os_sem, or_sem, hs_sem, hr_sem, gs_sem, gr_sem, ls_sem, lr_sem, xs_sem, xr_sem, es_sem, er_sem, keep_sem, table_sem,
+    hs_sem, hr_sem, gs_sem, gr_sem, ls_sem, lr_sem, xs_sem, xr_sem, es_sem, er_sem, keep_sem, table_sem, out_sem,
 ):
     n, chips, replicas = sizes
     z, r, c, y = place(sizes)
@@ -203,17 +203,21 @@
                 def _():
                     line(a, 0, k, way).start()
 
-    def mate_copy(src, dst, s, way):
-        w = 0 if way > 0 else 1
-        return remote(src, dst, ms_sem.at[w, s], mr_sem.at[w, s], mate)
-
     def mate_chunk(s, k, way):
-        return mate_copy(shard(cot_own, z - way * s, k), shard(cot_mate, z - way * s, k), s, way)
+        return remote(
+            shard(cot_own, z - way * s, k), shard(cot_mate, z - way * s, k),
+            ms_sem.at[0], mr_sem.at[0], mate,
+        )
+
+    def mate_chunks():
+        return remote(cot_own, cot_mate, ms_sem.at[0], mr_sem.at[0], mate)
 
     def mate_turned(s, way):
-        w = 0 if way > 0 else 1
         at = pl.ds((z - way * s) * blocks, blocks)
-        return remote(xt_own.at[at], xt_mate.at[at], ts_sem.at[w, s], tr_sem.at[w, s], mate)
+        return remote(xt_own.at[at], xt_mate.at[at], ts_sem.at[0], tr_sem.at[0], mate)
+
+    def mate_turns():
+        return remote(xt_own, xt_mate, ts_sem.at[0], tr_sem.at[0], mate)
 
     def turn(s, way):
         first = (z - way * s) * blocks
@@ -246,24 +250,6 @@
             @pl.when(has(s, way))
             def _():
                 turn(s, way)
-
-    def mate_chunks(act_on):
-        def each(s, way):
-            act_on(mate_copy(part_shard(cot_own, z - way * s), part_shard(cot_mate, z - way * s), s, way))
-
-        each(0, 1)
-        for s in range(1, n):
-            for way in (1, -1):
-                pl.when(has(s, way))(functools.partial(each, s, way))
-
-    def mate_turns(act_on):
-        act_on(mate_turned(0, 1))
-        for s in range(1, n):
-            for way in (1, -1):
-
-                @pl.when(has(s, way))
-                def _():
-                    act_on(mate_turned(s, way))
 
     def tile_range(full, r_of, q, k):
         return full.at[pl.ds((r_of * 2 + c) * per + q * part + k * weight_size, weight_size)]
@@ -287,24 +273,22 @@
 
     def core_copy(a, d, e, k):
         piece = tile_range(weights[a][1], from_chip(d), lax.rem(y - e + replicas, replicas), k)
-        return remote(piece, piece, cs_sem.at[a, d - 1, e], cr_sem.at[a, d - 1, e], mate)
+        return remote(piece, piece, cs_sem.at[a], cr_sem.at[a], mate)
 
     def share(full, r_of, q):
         return full.at[pl.ds((r_of * 2 + c) * per + q * part, part)]
 
-    def core_copies(a, d, e):
-        whole = share(weights[a][1], from_chip(d), lax.rem(y - e + replicas, replicas))
-        return remote(whole, whole, cs_sem.at[a, d - 1, e], cr_sem.at[a, d - 1, e], mate)
+    def core_copies(a):
+        whole = weights[a][1].at[pl.ds(0, chips * per)]
+        return remote(whole, whole, cs_sem.at[a], cr_sem.at[a], mate)
 
     def weights_sent(a):
-        own_core(a).wait_send()
+        core_copies(a).wait_send()
         for d in range(1, chips):
             remote(
                 weights[a][0].at[pl.ds(y * part, part)], share(weights[a][1], r, y),
                 ws_sem.at[a, d - 1], wr_sem.at[a, d - 1, 0], {"fsdp": lax.rem(r + d, chips) * 2 + c},
             ).wait_send()
-            for e in range(replicas):
-                core_copies(a, d, e).wait_send()
             for e in range(1, replicas):
                 whole = share(weights[a][1], from_chip(d), y)
                 remote(
@@ -314,7 +298,7 @@
 
     def own_core(a):
         return remote(
-            weights[a][0], weights[a][1].at[pl.ds(f * per, per)], os_sem.at[a], or_sem.at[a], mate
+            weights[a][0], weights[a][1].at[pl.ds(f * per, per)], cs_sem.at[a], cr_sem.at[a], mate
         )
 
     def w_event(a, k):
@@ -332,10 +316,7 @@
 
     def weights_in(a):
         weight_loads[a].wait()
-        own_core(a).wait_recv()
-        for d in range(1, chips):
-            for e in range(replicas):
-                core_copies(a, d, e).wait_recv()
+        core_copies(a).wait_recv()
 
     def hidden_mate(g):
         at = pl.ds(g * hidden_span, hidden_span)
@@ -381,7 +362,10 @@
         grad_mate(g).start()
 
     parts = (parts_o, parts_i)
-    outs = (out, inp)
+    outs = ((flat_o, out), (flat_i, inp))
+
+    def out_copy(a):
+        return pltpu.make_async_copy(outs[a][0], outs[a][1], out_sem.at[a])
     held = (held_r, held_l)
     pair_width = 4
 
@@ -459,7 +443,7 @@
 
     def finish(a):
         mine = part_shard(parts[a], z)
-        target = outs[a]
+        target = outs[a][0]
 
         def write(terms):
             for b in range(blocks):
@@ -487,6 +471,8 @@
         @pl.when(jnp.logical_and(z > 0, z < n - 1))
         def _():
             write((mine, held_r.at[a, n - 1 - z], held_l.at[a, z]))
+
+        out_copy(a).start()
 
     sums = (ga_d, ga_u)
     others = (gb_d, gb_u)
@@ -613,7 +599,7 @@
     cot_in = max(act_in + (n - 1) * SHARD_TIME, out_settle) + 1.0
 
     def cot_ready():
-        mate_chunks(lambda copy: copy.wait_recv())
+        mate_chunks().wait_recv()
         hidden_mates().wait_recv()
 
     at(cot_in, cot_ready)
@@ -627,7 +613,7 @@
         at(slope_from + 1.5 * g, slope_part, g)
 
     def grads_ready():
-        mate_turns(lambda copy: copy.wait_recv())
+        mate_turns().wait_recv()
         grad_mates().wait_recv()
 
     up_from = slope_from + 1.5 * PARTS + 1.0
@@ -661,9 +647,10 @@
     for work in steps:
         work()
 
-    mate_chunks(lambda copy: copy.wait_send())
-    mate_turns(lambda copy: copy.wait_send())
+    mate_chunks().wait_send()
+    mate_turns().wait_send()
     for a in range(2):
+        out_copy(a).wait()
         weights_sent(a)
         for way in (1, -1):
             for s in range(n - 1):
@@ -727,9 +714,11 @@
             + [jax.ShapeDtypeStruct((replicas - 1, per, 128, 128), kind)] * 2
         ),
         in_specs=[smem] * 4 + [vmem] * 4 + [anywhere] * 4,
-        out_specs=[vmem] * 2 + [anywhere] * 4,
+        out_specs=[anywhere] * 6,
         scratch_shapes=[
             held(model_blocks),
+            pltpu.VMEM((rows, features), kind),
+            pltpu.VMEM((rows, features), kind),
             pltpu.VMEM((model_blocks, 128, rows), kind),
             pltpu.VMEM((model_blocks, 128, rows), kind),
             held(model_blocks),
@@ -755,13 +744,12 @@
             dma((4,)),
             dma((2, 2, n - 1)),
             dma((2, 2, n - 1, CHUNKS)),
-            *twice(2, n),
-            *twice(2, n),
+            *twice(1),
+            *twice(1),
             dma((2, chips - 1)),
             dma((2, chips - 1, weight_chunks)),
             dma((2, chips - 1, replicas - 1)),
             dma((2, chips - 1, replicas - 1, weight_chunks)),
-            *twice(2, chips - 1, replicas),
             *twice(2),
             *twice(1),
             *twice(1),
@@ -771,6 +759,7 @@
             *twice(2, replicas - 1),
             dma((2,)),
             dma((2,)),
+            dma((2,)),
         ],
         compiler_params=pltpu.CompilerParams(
             collective_id=0, has_side_effects=True, vmem_limit_bytes=67043328
@@ -779,27 +768,33 @@
     )(*(v[:, 0] for v in lists), *(v.T for v in lists), activations, cotangent, up_tiles, down_tiles)
 
 
-def total_kernel(ga_u, gb_u, ga_d, gb_d, up_grad, down_grad):
+def total_kernel(ga_u, gb_u, ga_d, gb_d, out_in, inp_in, up_grad, down_grad, out, inp):
     for one, more, target in ((ga_u, gb_u, up_grad), (ga_d, gb_d, down_grad)):
         total = one[...].astype(jnp.float32)
         for e in range(more.shape[0]):
             total += more[e].astype(jnp.float32)
         target[...] = total
-
-
-def totals(ga_u, gb_u, ga_d, gb_d):
+    out[...] = out_in[...]
+    inp[...] = inp_in[...]
+
+
+def totals(ga_u, gb_u, ga_d, gb_d, out, inp):
     per = ga_u.shape[0]
     step = max(per // 2, 1)
+    rows, features = out.shape
     one = pl.BlockSpec((step, 128, 128), lambda i: (i, 0, 0))
     more = pl.BlockSpec((gb_u.shape[0], step, 128, 128), lambda i: (0, i, 0, 0))
+    flat = pl.BlockSpec((rows * step // per, features), lambda i: (i, 0))
     return pl.pallas_call(
         total_kernel,
         grid=(per // step,),
-        out_shape=[jax.ShapeDtypeStruct(ga_u.shape, jnp.float32)] * 2,
-        in_specs=[one, more, one, more],
-        out_specs=[one, one],
+        out_shape=(
+            [jax.ShapeDtypeStruct(ga_u.shape, jnp.float32)] * 2 + [jax.ShapeDtypeStruct(out.shape, out.dtype)] * 2
+        ),
+        in_specs=[one, more, one, more, flat, flat],
+        out_specs=[one, one, flat, flat],
         name="totals",
-    )(ga_u, gb_u, ga_d, gb_d)
+    )(ga_u, gb_u, ga_d, gb_d, out, inp)
 
 
 def body(sizes, activations, cotangent, up_tiles, down_tiles, up_rows, up_cols, down_rows, down_cols):
@@ -807,7 +802,7 @@
     out, inp, ga_u, ga_d, gb_u, gb_d = run_block(
         sizes, lists, activations, cotangent, up_tiles, down_tiles
     )
-    up_grad, down_grad = totals(ga_u, gb_u, ga_d, gb_d)
+    up_grad, down_grad, out, inp = totals(ga_u, gb_u, ga_d, gb_d, out, inp)
     return out, inp, up_grad, down_grad
 
 

time: 185 us -> 180 us (0.973)
  Pallas kernels: 183 us -> 180 us
    pallas_call x1, Pallas kernels: 177 us -> 173 us  [run_block(): pl.pallas_call(functools.partial(block_kernel, sizes), out_shape=[jax.Sha...]
where the time goes in v3:
time: 180 us
  Pallas kernels  180 us (100%)
    pallas_call x1, Pallas kernels, run_block(): pl.pallas_call(functools.partial(block_kernel, sizes), out_shape=[jax.Sha...  173 us
    pallas_call x1, Pallas kernels, totals(): pl.pallas_call(total_kernel, grid=(per // step,), out_shape=[jax.ShapeDty...  6.37 us

profile of v3, /device:TPU:0, one launch (start us, length us, event | category | flops | bytes accessed | tf_op | source)
XLA Modules:
  0.0 180.2 jit_solution(4895153448128443549)
XLA Ops:
  0.6 173.2 %block_all.1 = (bf16[128,2048]{1,0:T(8,128)(2,1)}, bf16[128,2048]{1,0:T(8,128)(2,1)}, bf16[64,128,128]{2,1,0:T(8,128)(2,1)}, bf16[64,128,128]{2,1,0:T(8,128)(2,1...) custom-call(s32[256]{0:T(256)} %bitcast.8, s32[256]{0:T(256)} %bitcast.10, s32[256]{0:T(256)} %bitcast.12, ...), custom_call_target="tpu_custom_call" | custom-call | tf_op jit(solution)/shard_map/block_all/pallas_call | solution.py:709
  173.8 6.4 %totals.1 = (f32[64,128,128]{2,1,0:T(8,128)}, f32[64,128,128]{2,1,0:T(8,128)}, bf16[128,2048]{1,0:T(8,128)(2,1)}, bf16[128,2048]{1,0:T(8,128)(2,1)}) custom-call(bf16[64,128,128]{2,1,0:T(8,128)(2,1)} %get-tuple-element.14.ga_u, bf16[1,64,128,128]{3,2,1,0:T(8,128)(2,1)} %get-tuple-element.15.gb_u, bf16[64,128,128]{2,1,0:T(8,128)(2,1)} %get-tuple-element.16.ga_d, ...), custom_call_target="tpu_custom_call" | custom-call | tf_op jit(solution)/shard_map/totals/pallas_call | solution.py:788

commit v4 on v3

--- a/solution.py
+++ b/solution.py
@@ -14,6 +14,14 @@
 WEIGHT_CHUNKS = 4
 PARTS = 8
 HIDDEN_PARTS = 4
+RELAY = 2
+INP_REST = 55.0
+FINISH = 100.0
+INP_LATE = 48.0
+FOLD_LATE = 2.0
+PASS_X = 24.0
+RELAYED = 42.0
+PASS_Y = 54.0
 LANES = 128
 
 SHARD_TIME = 11.3
@@ -53,7 +61,11 @@
     return z, f // 2, f % 2, y
 
 
-def enter(sizes):
+def relay_pieces(n, pieces):
+    return min(RELAY, pieces // 4) if n >= 4 else 0
+
+
+def enter(sizes, relays):
     n, chips, replicas = sizes
     z, r, c, y = place(sizes)
     barrier = pltpu.get_barrier_semaphore()
@@ -74,8 +86,20 @@
         greet({"fsdp": lax.rem(r + d, chips) * 2 + c})
     for e in range(1, replicas):
         greet({"dp": lax.rem(y + e, replicas)})
-    sides = jnp.where(z < n - 1, 1, 0) + jnp.where(z > 0, 1, 0)
-    pl.semaphore_wait(barrier, sides + 1 + (chips - 1) + (replicas - 1))
+    others = (chips - 1) + (replicas - 1)
+    awaited = jnp.where(z < n - 1, 1, 0) + jnp.where(z > 0, 1, 0) + 1 + others
+    if relays:
+
+        @pl.when(jnp.logical_or(z == 1, z == n - 2))
+        def _():
+            outer = jnp.where(z == 1, 0, n - 1)
+            for d in range(1, chips):
+                greet({"fsdp": lax.rem(r + d, chips) * 2 + c, "tensor": outer})
+            for e in range(1, replicas):
+                greet({"dp": lax.rem(y + e, replicas), "tensor": outer})
+
+        awaited += jnp.where(jnp.logical_or(z == 0, z == n - 1), others, 0)
+    pl.semaphore_wait(barrier, awaited)
 
 
 def padded(size):
@@ -129,9 +153,10 @@
     act, cot, up, down,
     out, inp, ga_u, ga_d, gb_u, gb_d,
     x_all, flat_o, flat_i, xt_own, xt_mate, cot_own, cot_mate, u_all, d_all, hidden, ht_own, ht_mate, slope,
-    pg_own, pg_mate, run, acc, parts_o, parts_i, held_r, held_l, stage, x_in, made, tables,
+    pg_own, pg_mate, run, acc, parts_o, parts_i, held_r, held_l, stage, x_in, relay_x, relay_y, made, tables,
     load_sem, zs_sem, zr_sem, ms_sem, mr_sem, ts_sem, tr_sem, ws_sem, wr_sem, ys_sem, yr_sem, cs_sem, cr_sem,
     hs_sem, hr_sem, gs_sem, gr_sem, ls_sem, lr_sem, xs_sem, xr_sem, es_sem, er_sem, keep_sem, table_sem, out_sem,
+    rs_sem, rr_sem, fs_sem, ts2_sem, tr2_sem, fs2_sem,
 ):
     n, chips, replicas = sizes
     z, r, c, y = place(sizes)
@@ -146,6 +171,11 @@
     weight_size = part // weight_chunks
     pieces = min(PIECES, per)
     size = per // pieces
+    relays = relay_pieces(n, pieces)
+    at_end = jnp.logical_or(z == 0, z == n - 1)
+    helps = jnp.logical_or(z == 1, z == n - 2)
+    inner = jnp.where(z == 0, 1, n - 2)
+    outer = jnp.where(z == 1, 0, n - 1)
     span = hidden_blocks // PARTS
     hidden_span = hidden_blocks // HIDDEN_PARTS
     features = (x_all, cot_own)
@@ -167,7 +197,7 @@
         weight_loads.append(copy)
     hidden[hidden_blocks] = jnp.zeros(hidden.shape[1:], hidden.dtype)
     pg_own[hidden_blocks] = jnp.zeros(pg_own.shape[1:], pg_own.dtype)
-    enter(sizes)
+    enter(sizes, relays)
 
     def part_shard(ref, s):
         return ref.at[pl.ds(s * blocks, blocks)]
@@ -413,12 +443,12 @@
             found = run[jnp.maximum(spot, 0)]
             target[b] = jnp.where(spot >= 0, found, jnp.zeros_like(found))
 
-        for i in range(n - 1):
-            for way in (1, -1):
-
-                @pl.when(edge(way))
-                def _():
-                    fold(a, i, way, True).start()
+    def fold_start(a, i):
+        for way in (1, -1):
+
+            @pl.when(edge(way))
+            def _():
+                fold(a, i, way, True).start()
 
     def add_into(target, terms):
         @pl.loop(0, target.shape[0])
@@ -519,10 +549,68 @@
             done_piece(a, k), sums[a].at[pl.ds(k * size, size)], keep_sem.at[a]
         )
 
+    def piece(k):
+        return pl.ds(k * size, size)
+
+    def x_out(d, where):
+        return remote(
+            stage.at[0, d - 1, where], relay_x.at[d - 1, where], rs_sem.at[d - 1], rr_sem.at[0, d - 1],
+            {"fsdp": lax.rem(r + d, chips) * 2 + c, "tensor": inner},
+        )
+
+    def x_out_piece(k, d):
+        return remote(
+            stage.at[0, d - 1, piece(k)], relay_x.at[d - 1, piece(k)], rs_sem.at[d - 1], rr_sem.at[k, d - 1],
+            {"fsdp": lax.rem(r + d, chips) * 2 + c, "tensor": inner},
+        )
+
+    def x_on(d, where, recv_sem):
+        return remote(
+            relay_x.at[d - 1, where], x_in.at[0, d - 1, where], fs_sem.at[d - 1], recv_sem, {"tensor": outer}
+        )
+
+    def y_out(e, where, recv_sem):
+        return remote(
+            x_in.at[0, 0, where], relay_y.at[e - 1, where], ts2_sem.at[e - 1], recv_sem,
+            {"dp": lax.rem(y + e, replicas), "tensor": inner},
+        )
+
+    def y_on(e, where):
+        return remote(
+            relay_y.at[e - 1, where], others[0].at[e - 1, where], fs2_sem.at[e - 1], er_sem.at[0, e - 1],
+            {"tensor": outer},
+        )
+
+    def hand_relays():
+        for k in range(relays):
+            for d in range(1, chips):
+                first = first_tile(lax.rem(r + d, chips), k)
+                values = [term(0, first + i) for i in range(size)]
+                for i in range(size):
+                    stage[0, d - 1, k * size + i] = values[i].astype(jnp.bfloat16)
+                x_out_piece(k, d).start()
+
+    def pass_x(k):
+        @pl.when(helps)
+        def _():
+            for d in range(1, chips):
+                x_out_piece(k, d).wait_recv()
+                x_on(d, piece(k), xr_sem.at[0, k, d - 1]).start()
+
+    def pass_y(k):
+        @pl.when(helps)
+        def _():
+            for e in range(1, replicas):
+                y_out(e, piece(k), tr2_sem.at[k, e - 1]).wait_recv()
+                y_on(e, piece(k)).start()
+
+    def relayed_event(k):
+        x_event(0, k, True)
+
     def x_events(a, first_piece, end):
         pl.loop(first_piece, end)(functools.partial(x_event, a))
 
-    def x_event(a, k):
+    def x_event(a, k, relayed=False):
         first = first_tile(r, k)
         values = [term(a, first + i) for i in range(size)]
         for d in range(1, chips):
@@ -533,13 +621,11 @@
                 total += x_in[a, d - 1, k * size + i].astype(jnp.float32)
             x_in[a, 0, k * size + i] = total.astype(jnp.bfloat16)
         for e in range(1, replicas):
-            e_copy(a, k, e).start()
+            if relayed:
+                y_out(e, piece(k), tr2_sem.at[k, e - 1]).start()
+            else:
+                e_copy(a, k, e).start()
         keep_copy(a, k).start()
-
-    plan = []
-
-    def at(time, work, *args):
-        plan.append((time, functools.partial(work, *args)))
 
     def start_all():
         loads[0].wait()
@@ -563,89 +649,129 @@
             made[t, pl.ds(row, 1), pl.ds(0, values.shape[1])] = values
         table_copy(t).start()
 
-    at(0.0, start_all)
-    for t in range(2):
-        at(10.2 + 5.65 * t, make_table, t)
-        at(24.0, lambda t: table_copy(t).wait(), t)
-    at(5.7, turn, 0, 1)
-    chunk_time = SHARD_TIME / CHUNKS
-    for s in range(1, n):
-        for k in range(CHUNKS):
-            when = 2.0 + ((s - 1) * CHUNKS + k + 1) * chunk_time
-            at(when, z_event, 0, s, k)
-        at(2.0 + s * SHARD_TIME + 0.1 + chunk_time, turn_event, s)
-    act_in = 2.0 + (n - 1) * SHARD_TIME
-    at(2.05 + max(n - 2, 0) * SHARD_TIME, z_start, 1)
-    for a in range(2):
-        for k in range(weight_chunks):
-            when = 2.2 + (a * weight_chunks + k + 1) * WEIGHT_TIME
-            at(when, w_event, a, k)
-            at(when + 1.2 * WEIGHT_TIME, y_event, a, k)
-    up_in = 2.3 + (weight_chunks + 1.2) * WEIGHT_TIME
-    down_in = 2.3 + (2 * weight_chunks + 1.2) * WEIGHT_TIME
-    at(up_in + 2.0, weights_in, 0)
-    at(down_in + 2.0, weights_in, 1)
-    hidden_from = max(act_in, up_in + 2.0) + 0.5
-    for g in range(HIDDEN_PARTS):
-        at(hidden_from + 3.0 * g, hidden_part, g)
-    out_from = max(hidden_from + 3.0 * HIDDEN_PARTS, down_in + 2.0) + 0.5
-    for g in range(HIDDEN_PARTS):
-        at(out_from + 2.4 * g, run_part, 0, g)
-    out_settle = out_from + 2.4 * HIDDEN_PARTS
-    at(out_settle, settle, 0)
-    for s in range(1, n):
-        for k in range(CHUNKS):
-            at(act_in + ((s - 1) * CHUNKS + k + 1) * chunk_time, z_event, 1, s, k)
-    cot_in = max(act_in + (n - 1) * SHARD_TIME, out_settle) + 1.0
+    def table_ready(t):
+        table_copy(t).wait()
 
     def cot_ready():
         mate_chunks().wait_recv()
         hidden_mates().wait_recv()
 
-    at(cot_in, cot_ready)
-    piece_time = 2 * SHARD_TIME * PIECE_SHARE / pieces
-    group = max(pieces // 8, 1)
-    at(cot_in + 0.1, hand_over, 0, 0, group)
-    for k in range(group, pieces, group):
-        at(cot_in + 0.2 + 1.2 * (k // group), hand_over, 0, k, min(k + group, pieces))
-    slope_from = cot_in + 9.0
-    for g in range(PARTS):
-        at(slope_from + 1.5 * g, slope_part, g)
-
     def grads_ready():
         mate_turns().wait_recv()
         grad_mates().wait_recv()
 
-    up_from = slope_from + 1.5 * PARTS + 1.0
-    at(up_from, grads_ready)
-    for k in range(0, pieces, group):
-        at(up_from + 0.1 + 1.4 * (k // group), hand_over, 1, k, min(k + group, pieces))
-    inp_from = up_from + 0.1 + 1.4 * 8
-    for g in range(PARTS):
-        at(inp_from + 1.5 * g, run_part, 1, g)
-    inp_settle = inp_from + 1.5 * PARTS
-    at(inp_settle, settle, 1)
-    for a, start in enumerate((out_settle, inp_settle)):
+    chunk_time = SHARD_TIME / CHUNKS
+    piece_time = 4 * SHARD_TIME / pieces
+    up_in = 2.3 + (weight_chunks + 1.2) * WEIGHT_TIME
+    down_in = 2.3 + (2 * weight_chunks + 1.2) * WEIGHT_TIME
+    group = max(pieces // 8, 1)
+    end_cot_in = 4.0 + 2 * (n - 1) * SHARD_TIME
+    end_inp_settle = end_cot_in + INP_LATE
+
+    def order(ends):
+        plan = []
+
+        def at(time, work, *args):
+            plan.append((time, functools.partial(work, *args)))
+
+        at(0.0, start_all)
+        for t in range(2):
+            at(10.2 + 5.65 * t, make_table, t)
+            at(24.0, table_ready, t)
+        at(5.7, turn, 0, 1)
+        hops = n - 1 if ends else max(n - 2, 1)
+        for s in range(1, n):
+            for k in range(CHUNKS):
+                at(2.0 + ((s - 1) * CHUNKS + k + 1) * chunk_time, z_event, 0, s, k)
+                at(2.0 + hops * SHARD_TIME + ((s - 1) * CHUNKS + k + 1) * chunk_time, z_event, 1, s, k)
+            at(2.0 + s * SHARD_TIME + 0.1 + chunk_time, turn_event, s)
+        at(2.05 + max(n - 2, 0) * SHARD_TIME, z_start, 1)
+        for a in range(2):
+            for k in range(weight_chunks):
+                when = 2.2 + (a * weight_chunks + k + 1) * WEIGHT_TIME
+                at(when, w_event, a, k)
+                at(when + 1.2 * WEIGHT_TIME, y_event, a, k)
+        at(up_in + 2.0, weights_in, 0)
+        at(down_in + 2.0, weights_in, 1)
+        hidden_from = max(2.0 + hops * SHARD_TIME, up_in + 2.0) + 0.5
+        hidden_in = hidden_from + 3.0 * HIDDEN_PARTS
+        for g in range(HIDDEN_PARTS):
+            at(hidden_from + 3.0 * g, hidden_part, g)
+        out_from = max(hidden_in, down_in + 2.0) + 0.5
+        out_settle = out_from + 2.4 * HIDDEN_PARTS
+        for g in range(HIDDEN_PARTS):
+            at(out_from + 2.4 * g, run_part, 0, g)
+        at(out_settle, settle, 0)
+        cot_in = 2.0 + 2 * hops * SHARD_TIME + 1.0
+        cot_in = max(cot_in, out_settle if ends else hidden_in) + 1.0
+        away = relays if ends else 0
+        at(cot_in, cot_ready)
+        if away:
+            at(cot_in + 0.05, hand_relays)
+        for j, k in enumerate(range(away, pieces, group)):
+            at(cot_in + 0.1 + 1.2 * j, hand_over, 0, k, min(k + group, pieces))
+        slope_from = max(cot_in + 9.0, out_settle + 0.5)
+        for g in range(PARTS):
+            at(slope_from + 1.5 * g, slope_part, g)
+        up_from = slope_from + 1.5 * PARTS + 1.0
+        at(up_from, grads_ready)
+        first_groups = 3 if ends else 8
+        inp_from = up_from + 0.1 + 1.4 * first_groups
+        for j, k in enumerate(range(0, pieces, group)):
+            late = 0.0 if j < first_groups else 0.7
+            at(up_from + 0.1 + 1.4 * j + late, hand_over, 1, k, min(k + group, pieces))
+        for g in range(PARTS):
+            at(inp_from + 1.5 * g, run_part, 1, g)
+        inp_settle = inp_from + 1.5 * PARTS + (3.0 if ends else 0.0)
+        at(inp_settle, settle, 1)
+        late = end_cot_in + FOLD_LATE
+        for i in range(n - 1):
+            at(max(out_settle, late if i and relays else 0.0) + 0.1, fold_start, 0, i)
+            at(max(inp_settle, end_cot_in + INP_REST if i and relays else 0.0) + 0.1, fold_start, 1, i)
         for t in range(1, n - 1):
-            at(start + 1.0 + t * SHARD_TIME, fold_event, a, t)
-        at(start + 3.0 + (n - 1) * SHARD_TIME, finish, a)
-    for a in range(2):
-        for k in range(pieces):
-            when = cot_in + 2.2 + piece_time * (a * pieces + k + 1)
-            at(max(when, up_from + 0.2) if a else when, x_event, a, k)
-
-    plan.sort(key=lambda item: item[0])
-    steps = []
-    for _, work in plan:
-        if work.func is x_event:
-            a, k = work.args
-            if steps and steps[-1].func is x_events and steps[-1].args[::2] == (a, k):
-                work = functools.partial(x_events, a, steps.pop().args[1], k + 1)
+            begin = max(out_settle, late + 4.0 if t > 1 and relays else 0.0)
+            at(begin + 1.0 + t * SHARD_TIME, fold_event, 0, t)
+            at(end_inp_settle + 1.0 + t * SHARD_TIME + (8.0 if t > 1 else 0.0), fold_event, 1, t)
+        at(late + 20.0 + (n - 1) * SHARD_TIME, finish, 0)
+        at(FINISH + end_inp_settle + 3.0 + (n - 1) * SHARD_TIME, finish, 1)
+        for k in range(relays):
+            if ends:
+                at(end_cot_in + RELAYED + piece_time * (k + 1), relayed_event, k)
             else:
-                work = functools.partial(x_events, a, k, k + 1)
-        steps.append(work)
-    for work in steps:
-        work()
+                at(end_cot_in + PASS_X + piece_time * (k + 1), pass_x, k)
+                at(end_cot_in + PASS_Y + piece_time * (k + 1), pass_y, k)
+        for a in range(2):
+            for k in range(0 if a else away, pieces):
+                when = cot_in + 2.2 + piece_time * (a * pieces + k - away + 1)
+                at(max(when, up_from + 0.2) if a else when, x_event, a, k)
+        plan.sort(key=lambda item: item[0])
+        steps = []
+        for _, work in plan:
+            if work.func is x_event:
+                a, k = work.args
+                if steps and steps[-1].func is x_events and steps[-1].args[::2] == (a, k):
+                    work = functools.partial(x_events, a, steps.pop().args[1], k + 1)
+                else:
+                    work = functools.partial(x_events, a, k, k + 1)
+            steps.append(work)
+        return steps
+
+    def run_all(steps):
+        for work in steps:
+            work()
+
+    end_steps, mid_steps = order(True), order(False)
+    if relays:
+        shared = 0
+        for one, other in zip(end_steps, mid_steps):
+            if (one.func, one.args) != (other.func, other.args):
+                break
+            shared += 1
+        run_all(end_steps[:shared])
+        pl.when(at_end)(functools.partial(run_all, end_steps[shared:]))
+        pl.when(jnp.logical_not(at_end))(functools.partial(run_all, mid_steps[shared:]))
+    else:
+        run_all(end_steps)
 
     mate_chunks().wait_send()
     mate_turns().wait_send()
@@ -668,18 +794,50 @@
 
     hidden_mates().wait_send()
     grad_mates().wait_send()
-    for a in range(2):
+    def sent(a, first):
+        where = pl.ds(first * size, per - first * size)
         for d in range(1, chips):
             remote(
-                stage.at[a, d - 1], x_in.at[a, d - 1], xs_sem.at[a, d - 1], xr_sem.at[a, 0, d - 1],
+                stage.at[a, d - 1, where], x_in.at[a, d - 1, where], xs_sem.at[a, d - 1], xr_sem.at[a, 0, d - 1],
                 {"fsdp": lax.rem(r + d, chips) * 2 + c},
             ).wait_send()
+        for e in range(1, replicas):
+            remote(
+                x_in.at[a, 0, where], others[a].at[e - 1, where], es_sem.at[a, e - 1], er_sem.at[a, e - 1],
+                {"dp": lax.rem(y + e, replicas)},
+            ).wait_send()
+
+    for a in range(2):
         pltpu.make_async_copy(x_in.at[a, 0], sums[a], keep_sem.at[a]).wait()
         for e in range(1, replicas):
             remote(
                 x_in.at[a, 0], others[a].at[e - 1], es_sem.at[a, e - 1], er_sem.at[a, e - 1],
                 {"dp": lax.rem(y + e, replicas)},
-            ).wait()
+            ).wait_recv()
+    sent(1, 0)
+    if not relays:
+        sent(0, 0)
+    else:
+        relayed = pl.ds(0, relays * size)
+
+        @pl.when(at_end)
+        def _():
+            sent(0, relays)
+            for d in range(1, chips):
+                x_out(d, relayed).wait_send()
+            for e in range(1, replicas):
+                y_out(e, relayed, tr2_sem.at[0, e - 1]).wait_send()
+
+        @pl.when(jnp.logical_not(at_end))
+        def _():
+            sent(0, 0)
+
+        @pl.when(helps)
+        def _():
+            for d in range(1, chips):
+                x_on(d, relayed, xr_sem.at[0, 0, d - 1]).wait_send()
+            for e in range(1, replicas):
+                y_on(e, relayed).wait_send()
 
 
 def run_block(sizes, lists, activations, cotangent, up_tiles, down_tiles):
@@ -694,6 +852,8 @@
     part = per // replicas
     weight_chunks = min(WEIGHT_CHUNKS, part)
     pieces = min(PIECES, per)
+    relays = max(relay_pieces(n, pieces), 1)
+    relayed = relays * per // pieces
     kind = jnp.bfloat16
     dma = pltpu.SemaphoreType.DMA
     vmem = pl.BlockSpec(memory_space=pltpu.VMEM)
@@ -739,6 +899,8 @@
             held(2, n - 1, blocks),
             pltpu.VMEM((2, chips - 1, per, 128, 128), kind),
             pltpu.VMEM((2, chips - 1, per, 128, 128), kind),
+            pltpu.VMEM((chips - 1, relayed, 128, 128), kind),
+            pltpu.VMEM((replicas - 1, relayed, 128, 128), kind),
             pltpu.VMEM((2, 8, padded(total_tiles + model_blocks)), jnp.int32),
             pltpu.SMEM((2, 8, padded(total_tiles + model_blocks)), jnp.int32),
             dma((4,)),
@@ -760,6 +922,12 @@
             dma((2,)),
             dma((2,)),
             dma((2,)),
+            dma((chips - 1,)),
+            dma((relays, chips - 1)),
+            dma((chips - 1,)),
+            dma((replicas - 1,)),
+            dma((relays, replicas - 1)),
+            dma((replicas - 1,)),
         ],
         compiler_params=pltpu.CompilerParams(
             collective_id=0, has_side_effects=True, vmem_limit_bytes=67043328

time: 180 us -> 178 us (0.989)
  Pallas kernels: 180 us -> 177 us
    pallas_call x1, Pallas kernels: 173 us -> 171 us  [run_block(): pl.pallas_call(functools.partial(block_kernel, sizes), out_shape=[jax.Sha...]
where the time goes in v4:
time: 178 us
  Pallas kernels  177 us (99%)
    pallas_call x1, Pallas kernels, run_block(): pl.pallas_call(functools.partial(block_kernel, sizes), out_shape=[jax.Sha...  171 us
    pallas_call x1, Pallas kernels, totals(): pl.pallas_call(total_kernel, grid=(per // step,), out_shape=[jax.ShapeDty...  6.37 us

profile of v4, /device:TPU:0, one launch (start us, length us, event | category | flops | bytes accessed | tf_op | source)
XLA Modules:
  0.0 177.7 jit_solution(4128338489753646904)
XLA Ops:
  0.6 170.6 %block_all.1 = (bf16[128,2048]{1,0:T(8,128)(2,1)}, bf16[128,2048]{1,0:T(8,128)(2,1)}, bf16[64,128,128]{2,1,0:T(8,128)(2,1)}, bf16[64,128,128]{2,1,0:T(8,128)(2,1...) custom-call(s32[256]{0:T(256)} %bitcast.8, s32[256]{0:T(256)} %bitcast.10, s32[256]{0:T(256)} %bitcast.12, ...), custom_call_target="tpu_custom_call" | custom-call | tf_op jit(solution)/shard_map/block_all/pallas_call | solution.py:869
  171.2 6.4 %totals.1 = (f32[64,128,128]{2,1,0:T(8,128)}, f32[64,128,128]{2,1,0:T(8,128)}, bf16[128,2048]{1,0:T(8,128)(2,1)}, bf16[128,2048]{1,0:T(8,128)(2,1)}) custom-call(bf16[64,128,128]{2,1,0:T(8,128)(2,1)} %get-tuple-element.14.ga_u, bf16[1,64,128,128]{3,2,1,0:T(8,128)(2,1)} %get-tuple-element.15.gb_u, bf16[64,128,128]{2,1,0:T(8,128)(2,1)} %get-tuple-element.16.ga_d, ...), custom_call_target="tpu_custom_call" | custom-call | tf_op jit(solution)/shard_map/totals/pallas_call | solution.py:956

commit v5 on v4

--- a/solution.py
+++ b/solution.py
@@ -11,7 +11,7 @@
 COL_TILES = 8
 PIECES = 16
 CHUNKS = 2
-WEIGHT_CHUNKS = 4
+WEIGHT_CHUNKS = 8
 PARTS = 8
 HIDDEN_PARTS = 4
 RELAY = 2
@@ -25,7 +25,7 @@
 LANES = 128
 
 SHARD_TIME = 11.3
-WEIGHT_TIME = 5.6
+WEIGHT_TIME = 2.8
 PIECE_SHARE = 2
 
 inv_root_two = 0.7071067811865476

time: 178 us -> 180 us (1.011)
  Pallas kernels: 177 us -> 179 us
    pallas_call x1, Pallas kernels: 171 us -> 173 us  [run_block(): pl.pallas_call(functools.partial(block_kernel, sizes), out_shape=[jax.Sha...]
where the time goes in v5:
time: 180 us
  Pallas kernels  179 us (99%)
    pallas_call x1, Pallas kernels, run_block(): pl.pallas_call(functools.partial(block_kernel, sizes), out_shape=[jax.Sha...  173 us
    pallas_call x1, Pallas kernels, totals(): pl.pallas_call(total_kernel, grid=(per // step,), out_shape=[jax.ShapeDty...  6.37 us

profile of v5, /device:TPU:0, one launch (start us, length us, event | category | flops | bytes accessed | tf_op | source)
XLA Modules:
  0.0 180.0 jit_solution(11000264426009230858)
XLA Ops:
  0.6 172.8 %block_all.1 = (bf16[128,2048]{1,0:T(8,128)(2,1)}, bf16[128,2048]{1,0:T(8,128)(2,1)}, bf16[64,128,128]{2,1,0:T(8,128)(2,1)}, bf16[64,128,128]{2,1,0:T(8,128)(2,1...) custom-call(s32[256]{0:T(256)} %bitcast.8, s32[256]{0:T(256)} %bitcast.10, s32[256]{0:T(256)} %bitcast.12, ...), custom_call_target="tpu_custom_call" | custom-call | tf_op jit(solution)/shard_map/block_all/pallas_call | solution.py:869
  173.4 6.4 %totals.1 = (f32[64,128,128]{2,1,0:T(8,128)}, f32[64,128,128]{2,1,0:T(8,128)}, bf16[128,2048]{1,0:T(8,128)(2,1)}, bf16[128,2048]{1,0:T(8,128)(2,1)}) custom-call(bf16[64,128,128]{2,1,0:T(8,128)(2,1)} %get-tuple-element.14.ga_u, bf16[1,64,128,128]{3,2,1,0:T(8,128)(2,1)} %get-tuple-element.15.gb_u, bf16[64,128,128]{2,1,0:T(8,128)(2,1)} %get-tuple-element.16.ga_d, ...), custom_call_target="tpu_custom_call" | custom-call | tf_op jit(solution)/shard_map/totals/pallas_call | solution.py:956
